TPU v7x, 128 devices: a whole 4x4x4 slice. The times are simulated.
128 devices in a mesh: users: 32 (over z, x, core), items: 4 (over y).
Axes of the slice: x: 4, y: 4, z: 4, core: 2. Of those that a mesh axis runs over, the one named last changes fastest.
Arguments:
- user_factors: bfloat16 [65536, 256], P('users'), may hold values from -1.5 to 1.5
- item_factors: bfloat16 [4, 4096, 256], P('items', 'users'), may hold values from -1.5 to 1.5
- confidence: bfloat16 [32, 4, 256, 128, 128], P('users', 'items'), may hold values from 0.099609375 to 10
- tile_counts: int32 [32, 4, 256], P('users', 'items'), may hold values from 1 to 4095
- tile_user: int32 [32, 4, 256], P('users', 'items'), may hold values from 0 to 15
- tile_item: int32 [32, 4, 256], P('users', 'items'), may hold values from 0 to 31
- block_slot: int32 [4, 32], P('items'), may hold values from 0 to 31, each once within a row
- live_tiles: int32 [32, 4], P('users', 'items'), may hold values from 64 to 256, as said below
Outputs:
- user_grad: float32 [65536, 256], P('users')
- item_grad: float32 [4, 4096, 256], P('items', 'users')
Inputs may be any that keep to these rules, and one draw needn't show every extreme that they name: Tile slots at positions from live_tiles on are ignored; some user shard and group uses all 256 slots.
All inputs are finite; a program needn't handle non-finite values.
Results may differ from a plain program's by a relative error of at most 0.0012.
Values may be sent and summed in bfloat16 or wider, within the bound.
No kernel may reach another device: no remote copies, remote signals or barrier semaphores. Data moves between devices by JAX's collectives and lax.ppermute only.
A program may use at most 128 MiB of HBM per device.

v0:
```python
import jax
import jax.numpy as jnp
from jax import lax
from jax.experimental import pallas as pl
from jax.experimental.pallas import tpu as pltpu
from jax.sharding import PartitionSpec as P


GRAD_SCALE = 0.005
GRAM_WEIGHT = 0.5
SLOTS = 8
GROUP = 4
UNROLL = 2
RING = 4
TAIL = 16
TOP = 32000.0


def dot(a, b, ca, cb):
    return lax.dot_general(a, b, (((ca,), (cb,)), ((), ())), preferred_element_type=jnp.float32)


def split(x):
    high = x.astype(jnp.bfloat16)
    return high, (x - high.astype(jnp.float32)).astype(jnp.bfloat16)


def encode(out_ref, x):
    rows = x.shape[0]
    top = jnp.max(jnp.abs(x), axis=0, keepdims=True)
    power = jnp.ceil(jnp.log2(jnp.maximum(top, 1e-30) * (1.0 / TOP)))
    out_ref[:rows, :] = jnp.round(x * jnp.exp2(-power)).astype(jnp.int32).astype(jnp.int16)
    tail = jnp.broadcast_to(power, (TAIL, x.shape[1]))
    out_ref[rows:, :] = tail.astype(jnp.int32).astype(jnp.int16)


def decode(ref):
    rows = ref.shape[0] - TAIL
    power = ref[rows:, :].astype(jnp.int32).astype(jnp.float32)[:1]
    return ref[:rows, :].astype(jnp.int32).astype(jnp.float32) * jnp.exp2(power)


def plan_kernel(here_ref, live_ref, user_ref, item_ref, count_ref, slot_ref, head_ref, pair_ref, tile_ref, panel_ref, factor_ref, group_ref, weight_ref, block_ref):
    tiles = user_ref.shape[1]
    spots = tile_ref.shape[1]
    panels = slot_ref.shape[1]
    z = here_ref[0] // 8
    x = (here_ref[0] // 2) & 3
    core = here_ref[0] & 1

    def grid(rows, lanes, axis):
        return lax.broadcasted_iota(jnp.int32, (rows, lanes), axis)

    down = grid(tiles, tiles, 0)
    across = grid(tiles, tiles, 1)

    def pick(mask, values, axis):
        return jnp.sum(jnp.where(mask, values, 0.0), axis=axis, keepdims=True)

    def column(row):
        return pick(down == across, row.astype(jnp.float32), 1)

    user_row = user_ref[...]
    user = column(user_row)
    user_int = user.astype(jnp.int32)
    order = grid(tiles, 1, 0)
    used = order < live_ref[0]
    rank = pick((user_int == user_row) & (across < down), jnp.ones((1, 1), jnp.float32), 1)
    own = (user_int == grid(tiles, 128, 1)) & used
    sizes = pick(own, jnp.ones((1, 1), jnp.float32), 0).astype(jnp.int32)
    groups = ((sizes + (GROUP - 1)) // GROUP).astype(jnp.float32)
    first = pick(grid(tiles, 128, 1) < user_int, groups, 1)
    spot = jnp.where(used, GROUP * first + rank, -1.0).astype(jnp.int32)
    item = column(item_ref[...]).astype(jnp.int32)
    slot = pick(item == grid(tiles, panels, 1), slot_ref[...].astype(jnp.float32), 1).astype(jnp.int32)
    far_z = (z - (slot >> 3)) & 3
    far_x = (x - (slot >> 1)) & 3
    odd = (slot & 1) == 1
    panel = ((core + slot) & 1) * 16 + jnp.where(odd, far_z * 4 + far_x, far_x * 4 + far_z)
    factor = jnp.log(1.0 + column(count_ref[...]))
    at = spot == grid(tiles, spots, 1)
    tile_ref[...] = pick(at, order.astype(jnp.float32), 0).astype(jnp.int32)
    panel_ref[...] = pick(at, panel.astype(jnp.float32), 0).astype(jnp.int32)
    factor_ref[...] = pick(at, factor, 0)
    pair_ref[...] = pick(spot == GROUP * grid(tiles, pair_ref.shape[1], 1), user, 0).astype(jnp.int32)
    total = jnp.sum(groups, axis=1, keepdims=True)
    empty = GROUP * total
    panel_row = pick(down == across, panel.astype(jnp.float32), 0).astype(jnp.int32)
    rank = pick((panel == panel_row) & (across < down), jnp.ones((1, 1), jnp.float32), 1)
    own = (panel == grid(tiles, 128, 1)) & used
    sizes = pick(own, jnp.ones((1, 1), jnp.float32), 0).astype(jnp.int32)
    groups = ((sizes + (GROUP - 1)) // GROUP).astype(jnp.float32)
    first = pick(grid(tiles, 128, 1) < panel, groups, 1)
    place = jnp.where(used, GROUP * first + rank, -1.0).astype(jnp.int32)
    at = place == grid(tiles, spots, 1)
    weight_ref[...] = (pick(at, spot.astype(jnp.float32) - empty, 0) + empty).astype(jnp.int32)
    block_ref[...] = pick(at, user, 0).astype(jnp.int32)
    group_ref[...] = pick(place == GROUP * grid(tiles, 128, 1), panel.astype(jnp.float32), 0).astype(jnp.int32)
    lane = grid(1, 128, 1)
    item_total = jnp.sum(groups, axis=1, keepdims=True)
    numbers = jnp.where(lane == 0, total, item_total).astype(jnp.int32)
    rounded = (numbers + (UNROLL - 1)) // UNROLL * UNROLL
    head_ref[...] = jnp.where(lane == 1, here_ref[1], rounded)


def loads_of(piece_refs, items_ref, sems):
    return [
        pltpu.make_async_copy(piece, items_ref.at[pl.ds(RING * i, RING)], sems.at[i])
        for i, piece in enumerate(piece_refs)
    ]


def user_kernel(*refs):
    head_ref, pair_ref, tile_ref, panel_ref, factor_ref, users_ref, conf_ref = refs[:7]
    piece_refs = refs[7:15]
    user_own, user_1, user_2, user_3, weight_out = refs[15:20]
    items_ref, user_acc, conf_buf, weights_ref, sems, piece_sems, out_sems = refs[20:]
    edge = conf_buf.shape[2]
    rank = users_ref.shape[1]
    groups = head_ref[0, 0]
    y = head_ref[0, 1]

    loads = loads_of(piece_refs, items_ref, piece_sems)
    for c in loads:
        c.start()

    def fetch(p):
        slot = lax.rem(p, SLOTS)
        for k in range(GROUP):
            tile = tile_ref[0, GROUP * p + k]
            pltpu.make_async_copy(conf_ref.at[tile], conf_buf.at[slot, k], sems.at[slot]).start()

    def arrive(p):
        slot = lax.rem(p, SLOTS)
        pltpu.make_async_copy(conf_ref.at[pl.ds(0, GROUP)], conf_buf.at[slot], sems.at[slot]).wait()

    def leave(p):
        rows = pl.ds(GROUP * p, GROUP)
        return pltpu.make_async_copy(weights_ref.at[rows], weight_out.at[rows], out_sems.at[p])

    for s in range(SLOTS):
        fetch(s)

    item_gram = jnp.zeros((rank, rank), jnp.float32)
    for i, c in enumerate(loads):
        c.wait()
        rows = items_ref[RING * i:RING * (i + 1)].reshape(-1, rank)
        item_gram = item_gram + dot(rows, rows, 0, 0)
    high, low = split(GRAM_WEIGHT * item_gram)
    quarter = user_acc.shape[0] // RING
    for k in range(RING):
        q = pl.multiple_of(((y - k) & 3) * quarter, quarter)
        rows = users_ref[pl.ds(q, quarter), :]
        user_acc[k * quarter:(k + 1) * quarter, :] = dot(rows, high, 1, 0) + dot(rows, low, 1, 0)

    def prepare(g):
        slot = lax.rem(g, SLOTS)
        u = pl.multiple_of(pair_ref[0, g] * edge, edge)
        users = users_ref[pl.ds(u, edge), :]
        scores = []
        for j in range(GROUP // 2):
            v0 = panel_ref[0, GROUP * g + 2 * j]
            v1 = panel_ref[0, GROUP * g + 2 * j + 1]
            items = jnp.concatenate([items_ref[v0], items_ref[v1]], axis=0)
            scores.append(dot(users, items, 1, 1))
        for k in range(GROUP):
            part = scores[k // 2][:, (k % 2) * edge:(k % 2 + 1) * edge]
            weight = conf_buf[slot, k].astype(jnp.float32) * factor_ref[0, GROUP * g + k] * (part - 1.0)
            weights_ref[GROUP * g + k] = weight.astype(jnp.bfloat16)

    for j in range(UNROLL):
        arrive(j)
    for j in range(UNROLL):
        prepare(j)

    def visit(i, carry):
        base = i * UNROLL
        for j in range(UNROLL):
            arrive(base + UNROLL + j)
        for j in range(UNROLL):
            fetch(base + j + SLOTS)
            leave(base + j).start()
        terms = []
        for j in range(UNROLL):
            g = base + j
            items = jnp.concatenate([items_ref[panel_ref[0, GROUP * g + k]] for k in range(GROUP)], axis=0)
            weights = jnp.concatenate([weights_ref[GROUP * g + k] for k in range(GROUP)], axis=1)
            terms.append(dot(weights, items, 1, 0))
        for j in range(UNROLL):
            prepare(base + UNROLL + j)
        for j in range(UNROLL):
            b = pair_ref[0, base + j]
            r = pl.multiple_of(((((y - (b >> 2)) & 3) << 2) + (b & 3)) * edge, edge)
            user_acc[pl.ds(r, edge), :] += terms[j]
        return carry

    lax.fori_loop(0, groups // UNROLL, visit, 0)
    for j in range(UNROLL):
        leave(groups + j).start()
    for j in range(UNROLL, SLOTS):
        arrive(groups + j)
    user_own[...] = user_acc[:quarter, :]
    for k, out in enumerate((user_1, user_2, user_3)):
        encode(out, user_acc[(k + 1) * quarter:(k + 2) * quarter, :])

    def drain(p, carry):
        leave(p).wait()
        return carry

    lax.fori_loop(0, groups + UNROLL, drain, 0)


def item_kernel(*refs):
    head_ref, group_ref, spot_ref, block_ref, users_ref, weight_ref = refs[:6]
    piece_refs = refs[6:14]
    item_own, item_0, item_1, item_2, item_3 = refs[14:19]
    items_ref, item_acc, buf, sems, piece_sems = refs[19:]
    edge = buf.shape[2]
    rank = users_ref.shape[1]
    groups = head_ref[0, 2]

    loads = loads_of(piece_refs, items_ref, piece_sems)
    for c in loads:
        c.start()

    def fetch(p):
        slot = lax.rem(p, SLOTS)
        for k in range(GROUP):
            spot = spot_ref[0, GROUP * p + k]
            pltpu.make_async_copy(weight_ref.at[spot], buf.at[slot, k], sems.at[slot]).start()

    def arrive(p):
        slot = lax.rem(p, SLOTS)
        pltpu.make_async_copy(weight_ref.at[pl.ds(0, GROUP)], buf.at[slot], sems.at[slot]).wait()

    ahead = SLOTS - UNROLL
    for s in range(ahead):
        fetch(s)

    item_acc[...] = jnp.zeros(item_acc.shape, jnp.float32)
    user_gram = dot(users_ref[...], users_ref[...], 0, 0)
    high, low = split(GRAM_WEIGHT * user_gram)

    def visit(i, carry):
        base = i * UNROLL
        for j in range(UNROLL):
            arrive(base + j)
        for j in range(UNROLL):
            fetch(base + j + ahead)

        terms = []
        for j in range(UNROLL):
            g = base + j
            parts = []
            for k in range(GROUP):
                u = pl.multiple_of(block_ref[0, GROUP * g + k] * edge, edge)
                parts.append(users_ref[pl.ds(u, edge), :])
            weights = buf[lax.rem(g, SLOTS)].reshape(GROUP * edge, edge)
            terms.append(dot(weights, jnp.concatenate(parts, axis=0), 0, 0))
        for j in range(UNROLL):
            r = pl.multiple_of(group_ref[0, base + j] * edge, edge)
            item_acc[pl.ds(r, edge), :] += terms[j]
        return carry

    lax.fori_loop(0, groups // UNROLL, visit, 0)
    for j in range(ahead):
        arrive(groups + j)
    for c in loads:
        c.wait()
    part = item_0.shape[0] - TAIL
    for k, out in enumerate((None, None, None, None, item_0, item_1, item_2, item_3)):
        items = items_ref[RING * k:RING * (k + 1)].reshape(part, rank)
        total = item_acc[k * part:(k + 1) * part, :] + (dot(items, high, 1, 0) + dot(items, low, 1, 0))
        if out is None:
            item_own[k * part:(k + 1) * part, :] = total
        else:
            encode(out, total)


def user_sum_kernel(after_ref, own_ref, p1, p2, p3, out_ref):
    encode(out_ref, (own_ref[...] + decode(p1)) + (decode(p2) + decode(p3)))


def user_out_kernel(here_ref, p0, p1, p2, p3, out_ref):
    quarter = p0.shape[0] - TAIL
    for k, p in enumerate((p0, p1, p2, p3)):
        q = pl.multiple_of(((here_ref[1] - k) & 3) * quarter, quarter)
        out_ref[pl.ds(q, quarter), :] = GRAD_SCALE * decode(p)


def item_core_kernel(own_ref, c0, c1, c2, c3, own_out, p1, p2, p3):
    part = own_out.shape[0]
    own_out[...] = own_ref[:part, :] + decode(c0)
    for k, (c, out) in enumerate(((c1, p1), (c2, p2), (c3, p3))):
        encode(out, own_ref[(k + 1) * part:(k + 2) * part, :] + decode(c))


def item_mid_kernel(own_ref, c1, c2, c3, own_out, p1, p2, p3):
    part = own_out.shape[0]
    total = (own_ref[...] + decode(c1)) + (decode(c2) + decode(c3))
    own_out[...] = total[:part]
    for k, out in enumerate((p1, p2, p3)):
        encode(out, total[(k + 1) * part:(k + 2) * part])


def item_out_kernel(own_ref, p1, p2, p3, out_ref):
    out_ref[...] = GRAD_SCALE * ((own_ref[...] + decode(p1)) + (decode(p2) + decode(p3)))


def smem():
    return pl.BlockSpec(memory_space=pltpu.SMEM)


def vmem():
    return pl.BlockSpec(memory_space=pltpu.VMEM)


def anywhere():
    return pl.BlockSpec(memory_space=pl.ANY)


def f32(*shape):
    return jax.ShapeDtypeStruct(shape, jnp.float32)


def i32(*shape):
    return jax.ShapeDtypeStruct(shape, jnp.int32)


def bf16(*shape):
    return jax.ShapeDtypeStruct(shape, jnp.bfloat16)


def i16(*shape):
    return jax.ShapeDtypeStruct(shape, jnp.int16)


def local(user_factors, item_factors, confidence, tile_counts, tile_user, tile_item, block_slot, live_tiles):
    rows, rank = user_factors.shape
    tiles, edge = confidence.shape[2:4]
    blocks = rows // edge
    pairs = ((tiles + (GROUP - 1) * blocks) // GROUP + UNROLL - 1) // UNROLL * UNROLL + UNROLL
    users_size = lax.axis_size("users")
    items_size = lax.axis_size("items")
    spots = range(users_size)

    def along_y(a, k):
        return lax.ppermute(a, "items", [(i, (i + k) % items_size) for i in range(items_size)])

    def move(i, by_z, k):
        z, x, core = i // 8, i // 2 % 4, i % 2
        if by_z:
            z = (z + k) % 4
        else:
            x = (x + k) % 4
        return z * 8 + x * 2 + core

    def along_first(a, k):
        return lax.ppermute(a, "users", [(i, move(i, i % 2 == 0, k)) for i in spots])

    def along_second(a, k):
        return lax.ppermute(a, "users", [(i, move(i, i % 2 == 1, k)) for i in spots])

    def to_core(a):
        return lax.ppermute(a, "users", [(i, i ^ 1) for i in spots])

    where = lax.broadcasted_iota(jnp.int32, (2,), 0)
    here = jnp.where(where == 0, lax.axis_index("users"), lax.axis_index("items")).astype(jnp.int32)

    own = item_factors[0]
    first = [own] + [along_first(own, k) for k in (1, 2, 3)]
    spot_total = -(-(max(GROUP * pairs, tiles + (GROUP - 1) * users_size) + GROUP * (SLOTS + UNROLL)) // 128) * 128
    plan = pl.pallas_call(
        plan_kernel,
        out_shape=(i32(1, 128), i32(1, 128), i32(1, spot_total), i32(1, spot_total), f32(1, spot_total), i32(1, 128), i32(1, spot_total), i32(1, spot_total)),
        in_specs=[smem()] * 2 + [vmem()] * 4,
        out_specs=[vmem()] * 8,
        name="plan",
    )(here, live_tiles[0], tile_user[0], tile_item[0], tile_counts[0], block_slot)
    first = jnp.stack(first)
    first, plan = lax.optimization_barrier((first, plan))
    pieces = [first] + [along_second(first, k) for k in (1, 2, 3)]
    pieces += [to_core(a) for a in pieces]

    quarter = rows // 4
    panels = users_size
    half_rows = panels * edge // 2
    part = half_rows // 4
    head, pair, tile, panel, factor, group, spot, block = plan
    *user_parts, weights = pl.pallas_call(
        user_kernel,
        out_shape=(f32(quarter, rank),) + (i16(quarter + TAIL, rank),) * 3 + (bf16(GROUP * pairs, edge, edge),),
        in_specs=[smem()] * 5 + [vmem(), anywhere()] + [anywhere()] * 8,
        out_specs=[vmem()] * 4 + [anywhere()],
        scratch_shapes=[
            pltpu.VMEM((panels, edge, rank), jnp.bfloat16),
            pltpu.VMEM((rows, rank), jnp.float32),
            pltpu.VMEM((SLOTS, GROUP, edge, edge), jnp.bfloat16),
            pltpu.VMEM((GROUP * pairs, edge, edge), jnp.bfloat16),
            pltpu.SemaphoreType.DMA((SLOTS,)),
            pltpu.SemaphoreType.DMA((8,)),
            pltpu.SemaphoreType.DMA((pairs,)),
        ],
        name="tiles_user",
    )(head, pair, tile, panel, factor, user_factors, confidence[0, 0], *pieces)
    item_own, *item_parts = pl.pallas_call(
        item_kernel,
        out_shape=(f32(half_rows, rank),) + (i16(part + TAIL, rank),) * 4,
        in_specs=[smem()] * 4 + [vmem(), anywhere()] + [anywhere()] * 8,
        out_specs=[vmem()] * 5,
        scratch_shapes=[
            pltpu.VMEM((panels, edge, rank), jnp.bfloat16),
            pltpu.VMEM((panels * edge, rank), jnp.float32),
            pltpu.VMEM((SLOTS, GROUP, edge, edge), jnp.bfloat16),
            pltpu.SemaphoreType.DMA((SLOTS,)),
            pltpu.SemaphoreType.DMA((8,)),
        ],
        name="tiles_item",
    )(head, group, spot, block, user_factors, weights, *pieces)
    user_own, *user_parts = user_parts
    after = item_own

    item_parts = [to_core(a) for a in item_parts]
    user_parts = [along_y(a, -k) for k, a in zip((1, 2, 3), user_parts)]

    user_code = pl.pallas_call(
        user_sum_kernel,
        out_shape=i16(quarter + TAIL, rank),
        in_specs=[anywhere()] + [vmem()] * 4,
        out_specs=vmem(),
        name="user_sum",
    )(after, user_own, *user_parts)

    def item_stage(kernel, size, *ins):
        return pl.pallas_call(
            kernel,
            out_shape=(f32(size, rank),) + (i16(size + TAIL, rank),) * 3,
            in_specs=[vmem()] * len(ins),
            out_specs=[vmem()] * 4,
        )(*ins)

    item_own, *item_parts = item_stage(item_core_kernel, part, item_own, *item_parts)
    item_parts = [along_second(a, -k) for k, a in zip((1, 2, 3), item_parts)]
    user_codes = [user_code] + [along_y(user_code, k) for k in (1, 2, 3)]
    item_own, *item_parts = item_stage(item_mid_kernel, edge, item_own, *item_parts)
    item_parts = [along_first(a, -k) for k, a in zip((1, 2, 3), item_parts)]
    item_grad = pl.pallas_call(
        item_out_kernel,
        out_shape=f32(edge, rank),
        in_specs=[vmem()] * 4,
        out_specs=vmem(),
        name="item_out",
    )(item_own, *item_parts)
    user_grad = pl.pallas_call(
        user_out_kernel,
        out_shape=f32(rows, rank),
        in_specs=[smem()] + [vmem()] * 4,
        out_specs=vmem(),
        name="user_out",
    )(here, *user_codes)
    return user_grad, item_grad[None]


def solution(mesh):
    in_specs = (
        P("users", None),
        P("items", "users", None),
        P("users", "items", None, None, None),
        P("users", "items", None),
        P("users", "items", None),
        P("users", "items", None),
        P("items", None),
        P("users", "items"),
    )
    out_specs = (P("users", None), P("items", "users", None))

    return jax.shard_map(local, mesh=mesh, in_specs=in_specs, out_specs=out_specs, check_vma=False)
```

profile of v0, /device:TPU:7, one launch (start us, length us, event | category | flops | bytes accessed | tf_op | source)
XLA Modules:
  0.0 111.8 jit_solution(15398258770574229356)
XLA Ops:
  0.6 0.6 collective-permute-start.2
  1.2 0.7 collective-permute-start.1
  1.9 2.0 %collective-permute-start = (bf16[128,256]{1,0:T(8,128)(2,1)}, bf16[128,256]{1,0:T(8,128)(2,1)S(1)}, u32[]{:S(2)}, u32[]{:S(2)}) collective-permute-start(bf16[128,256]{1,0:T(8,128)(2,1)} %bitcast.15), channel_id=1, source_target_pairs={{0,32},{4,12},{8,40},{12,20},{16,48},{20,28},{24,56},{28,4},{32,64... | collective-permute-start | bytes 196616 | tf_op jit(solution)/shard_map/ppermute | solution.py:359
  4.5 0.5 compare_select_fusion.here_ref
  5.1 2.1 %plan.1 = (s32[1,128]{1,0:T(1,128)}, s32[1,128]{1,0:T(1,128)}, s32[1,512]{1,0:T(1,128)}, s32[1,512]{1,0:T(1,128)}, f32[1,512]{1,0:T(1,128)}, /*index=5*/s32[1,12...) custom-call(s32[2]{0:T(128)} %compare_select_fusion.here_ref, s32[1]{0:T(128)} %bitcast.10.live_ref, s32[1,256]{1,0:T(1,128)} %bitcast.19, ...), custom_call_target="tpu_custom_call" | custom-call | tf_op jit(solution)/shard_map/plan/pallas_call | solution.py:373
  7.2 0.9 pad_maximum_fusion.refs_7_.refs_6_
  8.1 3.8 %collective-permute-start.5 = (bf16[4,128,256]{2,1,0:T(8,128)(2,1)S(1)}, bf16[4,128,256]{2,1,0:T(8,128)(2,1)S(1)}, u32[]{:S(2)}, u32[]{:S(2)}) collective-permute-start(bf16[4,128,256]{2,1,0:T(8,128)(2,1)S(1)} %pad_maximum_fusion.refs_7_.refs_6_), channel_id=1, source_target_pairs={{0,24},{4,100},{8,0},{12,108},{16,8},{20,116},{24,16},{28,124},{32... | collective-permute-start | bytes 786440 | tf_op jit(solution)/shard_map/ppermute | solution.py:362
  11.9 0.7 collective-permute-start.3
  12.6 4.2 %collective-permute-start.6 = (bf16[4,128,256]{2,1,0:T(8,128)(2,1)S(1)}, bf16[4,128,256]{2,1,0:T(8,128)(2,1)S(1)}, u32[]{:S(2)}, u32[]{:S(2)}) collective-permute-start(bf16[4,128,256]{2,1,0:T(8,128)(2,1)S(1)} %pad_maximum_fusion.refs_7_.refs_6_), channel_id=1, source_target_pairs={{0,4},{4,0},{8,12},{12,8},{16,20},{20,16},{24,28},{28,24},{32,36},... | collective-permute-start | bytes 786440 | tf_op jit(solution)/shard_map/ppermute | solution.py:365
  16.8 1.3 %collective-permute-done.5.refs_10_.refs_9_ = bf16[4,128,256]{2,1,0:T(8,128)(2,1)S(1)} collective-permute-done((bf16[4,128,256]{2,1,0:T(8,128)(2,1)S(1)}, bf16[4,128,256]{2,1,0:T(8,128)(2,1)S(1)}, u32[]{:S(2)}, u32[]{:S(2)}) %collective-permute-start.5) | collective-permute-done | bytes 262176 | tf_op jit(solution)/shard_map/ppermute | solution.py:362
  18.1 5.1 %collective-permute-start.9 = (bf16[4,128,256]{2,1,0:T(8,128)(2,1)S(1)}, bf16[4,128,256]{2,1,0:T(8,128)(2,1)S(1)}, u32[]{:S(2)}, u32[]{:S(2)}) collective-permute-start(bf16[4,128,256]{2,1,0:T(8,128)(2,1)S(1)} %collective-permute-done.5.refs_10_.refs_9_), channel_id=1, source_target_pairs={{0,4},{4,0},{8,12},{12,8},{16,20},{20,16},{24,28},{28,24},{32,36},... | collective-permute-start | bytes 786440 | tf_op jit(solution)/shard_map/ppermute | solution.py:365
  23.2 0.1 collective-permute-start.8
  23.3 0.8 collective-permute-start.7
  24.1 0.3 collective-permute-done.9.refs_14_.refs_13_
  24.3 0.4 collective-permute-done.8.refs_13_.refs_12_
  24.7 0.5 collective-permute-done.7.refs_12_.refs_11_
  25.3 0.2 copy-done.6
  25.4 0.5 copy-done.7
  25.9 23.9 %tiles_user.1 = (f32[512,256]{1,0:T(8,128)}, s16[528,256]{1,0:T(8,128)(2,1)}, s16[528,256]{1,0:T(8,128)(2,1)}, s16[528,256]{1,0:T(8,128)(2,1)}, bf16[312,128,128]{2,1,0:T(8,128)(2,1)}) custom-call(s32[1,128]{1,0:T(1,128)} %get-tuple-element.45.refs_0_, s32[1,128]{1,0:T(1,128)} %get-tuple-element.49.refs_1_, s32[1,512]{1,0:T(1,128)} %get-tuple-element.50.refs_2_, ...), custom_call_target="tpu_custom_call" | custom-call | tf_op jit(solution)/shard_map/tiles_user/pallas_call | solution.py:390
  49.9 16.8 %tiles_item.1 = (f32[2048,256]{1,0:T(8,128)}, s16[528,256]{1,0:T(8,128)(2,1)}, s16[528,256]{1,0:T(8,128)(2,1)}, s16[528,256]{1,0:T(8,128)(2,1)}, s16[528,256]{1,0:T(8,128)(2,1)}) custom-call(s32[1,128]{1,0:T(1,128)} %get-tuple-element.45.refs_0_, s32[1,128]{1,0:T(1,128)} %get-tuple-element.46.refs_1_, s32[1,512]{1,0:T(1,128)} %get-tuple-element.47.refs_2_, ...), custom_call_target="tpu_custom_call" | custom-call | tf_op jit(solution)/shard_map/tiles_item/pallas_call | solution.py:406
  66.7 0.1 collective-permute-start.16
  66.8 0.5 collective-permute-start.17
  67.3 0.1 collective-permute-start.18
  67.4 0.4 collective-permute-start.19
  67.8 3.8 %collective-permute-start.10 = (s16[528,256]{1,0:T(8,128)(2,1)S(1)}, s16[528,256]{1,0:T(8,128)(2,1)S(1)}, u32[]{:S(2)}, u32[]{:S(2)}) collective-permute-start(s16[528,256]{1,0:T(8,128)(2,1)S(1)} %copy-done.26), channel_id=1, source_target_pairs={{0,3},{1,0},{2,1},{3,2},{4,7},{5,4},{6,5},{7,6},{8,11},{9,8},{10,9... | collective-permute-start | bytes 811016 | tf_op jit(solution)/shard_map/ppermute | solution.py:348
  71.6 0.1 collective-permute-start.11
  71.7 1.3 %collective-permute-start.12 = (s16[528,256]{1,0:T(8,128)(2,1)S(1)}, s16[528,256]{1,0:T(8,128)(2,1)S(1)}, u32[]{:S(2)}, u32[]{:S(2)}) collective-permute-start(s16[528,256]{1,0:T(8,128)(2,1)S(1)} %copy-done.24), channel_id=1, source_target_pairs={{0,1},{1,2},{2,3},{3,0},{4,5},{5,6},{6,7},{7,4},{8,9},{9,10},{10,1... | collective-permute-start | bytes 811016 | tf_op jit(solution)/shard_map/ppermute | solution.py:348
  73.0 0.7 copy-done.13
  73.6 0.1 copy-done.14
  73.7 3.3 %shard_map.95 = (f32[512,256]{1,0:T(8,128)}, s16[528,256]{1,0:T(8,128)(2,1)}, s16[528,256]{1,0:T(8,128)(2,1)}, s16[528,256]{1,0:T(8,128)(2,1)}) custom-call(f32[2048,256]{1,0:T(8,128)} %get-tuple-element.55.after_ref.own_ref, s16[528,256]{1,0:T(8,128)(2,1)} %copy-done.11, s16[528,256]{1,0:T(8,128)(2,1)} %copy-done.12, s16[528,256]{1,0:T(8,128)(2,1)} %copy-done.13, ...), custom_call_target="tpu_custom_call" | custom-call | tf_op jit(solution)/shard_map/pallas_call | solution.py:435
  77.1 0.6 collective-permute-start.21
  77.7 5.4 %collective-permute-done.10.p1 = s16[528,256]{1,0:T(8,128)(2,1)S(1)} collective-permute-done((s16[528,256]{1,0:T(8,128)(2,1)S(1)}, s16[528,256]{1,0:T(8,128)(2,1)S(1)}, u32[]{:S(2)}, u32[]{:S(2)}) %collective-permute-start.10) | collective-permute-done | bytes 270368 | tf_op jit(solution)/shard_map/ppermute | solution.py:348
  83.1 3.9 %collective-permute-done.12.p3 = s16[528,256]{1,0:T(8,128)(2,1)S(1)} collective-permute-done((s16[528,256]{1,0:T(8,128)(2,1)S(1)}, s16[528,256]{1,0:T(8,128)(2,1)S(1)}, u32[]{:S(2)}, u32[]{:S(2)}) %collective-permute-start.12) | collective-permute-done | bytes 270368 | tf_op jit(solution)/shard_map/ppermute | solution.py:348
  87.0 0.7 copy-done.10
  87.7 2.3 %user_sum.1.p0 = s16[528,256]{1,0:T(8,128)(2,1)} custom-call(f32[2048,256]{1,0:T(8,128)} %get-tuple-element.55.after_ref.own_ref, f32[512,256]{1,0:T(8,128)} %get-tuple-element.56.own_ref, s16[528,256]{1,0:T(8,128)(2,1)} %copy-done.8, s16[528,256]{1,0:T(8,128)(2,1)} %copy-done.9, s16[528,256]{1,0:T(8,128)(2,1)} %copy-done.10), custom_call_target="tpu_custom_call" | custom-call | tf_op jit(solution)/shard_map/user_sum/pallas_call | solution.py:426
  90.0 0.4 collective-permute-start.14
  90.3 1.2 %collective-permute-start.13 = (s16[528,256]{1,0:T(8,128)(2,1)}, s16[528,256]{1,0:T(8,128)(2,1)S(1)}, u32[]{:S(2)}, u32[]{:S(2)}) collective-permute-start(s16[528,256]{1,0:T(8,128)(2,1)} %user_sum.1.p0), channel_id=1, source_target_pairs={{0,1},{1,2},{2,3},{3,0},{4,5},{5,6},{6,7},{7,4},{8,9},{9,10},{10,1... | collective-permute-start | bytes 811016 | tf_op jit(solution)/shard_map/ppermute | solution.py:348
  91.5 0.7 copy-done.16
  92.2 0.1 copy-done.17
  92.3 2.2 %shard_map.96 = (f32[128,256]{1,0:T(8,128)}, s16[144,256]{1,0:T(8,128)(2,1)}, s16[144,256]{1,0:T(8,128)(2,1)}, s16[144,256]{1,0:T(8,128)(2,1)}) custom-call(f32[512,256]{1,0:T(8,128)} %get-tuple-element.64.own_ref, s16[528,256]{1,0:T(8,128)(2,1)} %copy-done.15, s16[528,256]{1,0:T(8,128)(2,1)} %copy-done.16, s16[528,256]{1,0:T(8,128)(2,1)} %copy-done.17), custom_call_target="tpu_custom_call" | custom-call | tf_op jit(solution)/shard_map/pallas_call | solution.py:435
  94.5 0.6 collective-permute-start.24
  95.1 2.4 %collective-permute-done.15.p3 = s16[528,256]{1,0:T(8,128)(2,1)S(1)} collective-permute-done((s16[528,256]{1,0:T(8,128)(2,1)}, s16[528,256]{1,0:T(8,128)(2,1)S(1)}, u32[]{:S(2)}, u32[]{:S(2)}) %collective-permute-start.15) | collective-permute-done | bytes 270368 | tf_op jit(solution)/shard_map/ppermute | solution.py:348
  97.5 0.8 collective-permute-done.14.p2
  98.3 7.6 %collective-permute-done.13.p1 = s16[528,256]{1,0:T(8,128)(2,1)S(1)} collective-permute-done((s16[528,256]{1,0:T(8,128)(2,1)}, s16[528,256]{1,0:T(8,128)(2,1)S(1)}, u32[]{:S(2)}, u32[]{:S(2)}) %collective-permute-start.13) | collective-permute-done | bytes 270368 | tf_op jit(solution)/shard_map/ppermute | solution.py:348
  105.9 0.7 copy-done.20
  106.6 2.8 %user_out.1 = f32[2048,256]{1,0:T(8,128)} custom-call(s32[2]{0:T(128)} %compare_select_fusion.here_ref, s16[528,256]{1,0:T(8,128)(2,1)} %user_sum.1.p0, s16[528,256]{1,0:T(8,128)(2,1)} %copy-done.20, s16[528,256]{1,0:T(8,128)(2,1)} %copy-done.19, s16[528,256]{1,0:T(8,128)(2,1)} %copy-done.18), custom_call_target="tpu_custom_call" | custom-call | tf_op jit(solution)/shard_map/user_out/pallas_call | solution.py:454
  109.4 0.6 copy-done.21
  110.1 1.7 %item_out.1 = f32[128,256]{1,0:T(8,128)} custom-call(f32[128,256]{1,0:T(8,128)} %get-tuple-element.68.own_ref, s16[144,256]{1,0:T(8,128)(2,1)} %copy-done.21, s16[144,256]{1,0:T(8,128)(2,1)} %copy-done.22, s16[144,256]{1,0:T(8,128)(2,1)} %copy-done.23), custom_call_target="tpu_custom_call" | custom-call | tf_op jit(solution)/shard_map/item_out/pallas_call | solution.py:447
  (68 shorter events, 0.2 us)
Async XLA Ops:
  0.6 6.6 %collective-permute-start.2 = (bf16[128,256]{1,0:T(8,128)(2,1)}, bf16[128,256]{1,0:T(8,128)(2,1)S(1)}, u32[]{:S(2)}, u32[]{:S(2)}) collective-permute-start(bf16[128,256]{1,0:T(8,128)(2,1)} %bitcast.13), channel_id=1, source_target_pairs={{0,96},{4,28},{8,104},{12,4},{16,112},{20,12},{24,120},{28,20},{32... | collective-permute-start | bytes 196616 | tf_op jit(solution)/shard_map/ppermute | solution.py:359
  1.2 5.9 %collective-permute-start.1 = (bf16[128,256]{1,0:T(8,128)(2,1)}, bf16[128,256]{1,0:T(8,128)(2,1)S(1)}, u32[]{:S(2)}, u32[]{:S(2)}) collective-permute-start(bf16[128,256]{1,0:T(8,128)(2,1)} %bitcast.14), channel_id=1, source_target_pairs={{0,64},{4,20},{8,72},{12,28},{16,80},{20,4},{24,88},{28,12},{32,96... | collective-permute-start | bytes 196616 | tf_op jit(solution)/shard_map/ppermute | solution.py:359
  1.9 5.3 %collective-permute-start = (bf16[128,256]{1,0:T(8,128)(2,1)}, bf16[128,256]{1,0:T(8,128)(2,1)S(1)}, u32[]{:S(2)}, u32[]{:S(2)}) collective-permute-start(bf16[128,256]{1,0:T(8,128)(2,1)} %bitcast.15), channel_id=1, source_target_pairs={{0,32},{4,12},{8,40},{12,20},{16,48},{20,28},{24,56},{28,4},{32,64... | collective-permute-start | bytes 196616 | tf_op jit(solution)/shard_map/ppermute | solution.py:359
  8.1 17.1 %copy-start = (bf16[4,128,256]{2,1,0:T(8,128)(2,1)}, bf16[4,128,256]{2,1,0:T(8,128)(2,1)S(1)}, u32[]{:S(2)}) copy-start(bf16[4,128,256]{2,1,0:T(8,128)(2,1)S(1)} %pad_maximum_fusion.refs_7_.refs_6_) | copy-start | bytes 786436
  8.1 10.0 %collective-permute-start.5 = (bf16[4,128,256]{2,1,0:T(8,128)(2,1)S(1)}, bf16[4,128,256]{2,1,0:T(8,128)(2,1)S(1)}, u32[]{:S(2)}, u32[]{:S(2)}) collective-permute-start(bf16[4,128,256]{2,1,0:T(8,128)(2,1)S(1)} %pad_maximum_fusion.refs_7_.refs_6_), channel_id=1, source_target_pairs={{0,24},{4,100},{8,0},{12,108},{16,8},{20,116},{24,16},{28,124},{32... | collective-permute-start | bytes 786440 | tf_op jit(solution)/shard_map/ppermute | solution.py:362
  11.9 11.2 %collective-permute-start.4 = (bf16[4,128,256]{2,1,0:T(8,128)(2,1)S(1)}, bf16[4,128,256]{2,1,0:T(8,128)(2,1)S(1)}, u32[]{:S(2)}, u32[]{:S(2)}) collective-permute-start(bf16[4,128,256]{2,1,0:T(8,128)(2,1)S(1)} %pad_maximum_fusion.refs_7_.refs_6_), channel_id=1, source_target_pairs={{0,16},{4,68},{8,24},{12,76},{16,0},{20,84},{24,8},{28,92},{32,48}... | collective-permute-start | bytes 786440 | tf_op jit(solution)/shard_map/ppermute | solution.py:362
  11.9 11.3 %collective-permute-start.3 = (bf16[4,128,256]{2,1,0:T(8,128)(2,1)S(1)}, bf16[4,128,256]{2,1,0:T(8,128)(2,1)S(1)}, u32[]{:S(2)}, u32[]{:S(2)}) collective-permute-start(bf16[4,128,256]{2,1,0:T(8,128)(2,1)S(1)} %pad_maximum_fusion.refs_7_.refs_6_), channel_id=1, source_target_pairs={{0,8},{4,36},{8,16},{12,44},{16,24},{20,52},{24,0},{28,60},{32,40}... | collective-permute-start | bytes 786440 | tf_op jit(solution)/shard_map/ppermute | solution.py:362
  12.6 11.4 %collective-permute-start.6 = (bf16[4,128,256]{2,1,0:T(8,128)(2,1)S(1)}, bf16[4,128,256]{2,1,0:T(8,128)(2,1)S(1)}, u32[]{:S(2)}, u32[]{:S(2)}) collective-permute-start(bf16[4,128,256]{2,1,0:T(8,128)(2,1)S(1)} %pad_maximum_fusion.refs_7_.refs_6_), channel_id=1, source_target_pairs={{0,4},{4,0},{8,12},{12,8},{16,20},{20,16},{24,28},{28,24},{32,36},... | collective-permute-start | bytes 786440 | tf_op jit(solution)/shard_map/ppermute | solution.py:365
  18.1 7.2 %copy-start.1 = (bf16[4,128,256]{2,1,0:T(8,128)(2,1)}, bf16[4,128,256]{2,1,0:T(8,128)(2,1)S(1)}, u32[]{:S(2)}) copy-start(bf16[4,128,256]{2,1,0:T(8,128)(2,1)S(1)} %collective-permute-done.5.refs_10_.refs_9_) | copy-start | bytes 786436
  18.1 6.3 %collective-permute-start.9 = (bf16[4,128,256]{2,1,0:T(8,128)(2,1)S(1)}, bf16[4,128,256]{2,1,0:T(8,128)(2,1)S(1)}, u32[]{:S(2)}, u32[]{:S(2)}) collective-permute-start(bf16[4,128,256]{2,1,0:T(8,128)(2,1)S(1)} %collective-permute-done.5.refs_10_.refs_9_), channel_id=1, source_target_pairs={{0,4},{4,0},{8,12},{12,8},{16,20},{20,16},{24,28},{28,24},{32,36},... | collective-permute-start | bytes 786440 | tf_op jit(solution)/shard_map/ppermute | solution.py:365
  23.2 2.1 %copy-start.2 = (bf16[4,128,256]{2,1,0:T(8,128)(2,1)}, bf16[4,128,256]{2,1,0:T(8,128)(2,1)S(1)}, u32[]{:S(2)}) copy-start(bf16[4,128,256]{2,1,0:T(8,128)(2,1)S(1)} %collective-permute-done.4.refs_9_.refs_8_) | copy-start | bytes 786436
  23.2 1.5 %collective-permute-start.8 = (bf16[4,128,256]{2,1,0:T(8,128)(2,1)S(1)}, bf16[4,128,256]{2,1,0:T(8,128)(2,1)S(1)}, u32[]{:S(2)}, u32[]{:S(2)}) collective-permute-start(bf16[4,128,256]{2,1,0:T(8,128)(2,1)S(1)} %collective-permute-done.4.refs_9_.refs_8_), channel_id=1, source_target_pairs={{0,4},{4,0},{8,12},{12,8},{16,20},{20,16},{24,28},{28,24},{32,36},... | collective-permute-start | bytes 786440 | tf_op jit(solution)/shard_map/ppermute | solution.py:365
  23.3 2.0 %copy-start.3 = (bf16[4,128,256]{2,1,0:T(8,128)(2,1)}, bf16[4,128,256]{2,1,0:T(8,128)(2,1)S(1)}, u32[]{:S(2)}) copy-start(bf16[4,128,256]{2,1,0:T(8,128)(2,1)S(1)} %collective-permute-done.3.refs_8_.refs_7_) | copy-start | bytes 786436
  23.3 2.0 %collective-permute-start.7 = (bf16[4,128,256]{2,1,0:T(8,128)(2,1)S(1)}, bf16[4,128,256]{2,1,0:T(8,128)(2,1)S(1)}, u32[]{:S(2)}, u32[]{:S(2)}) collective-permute-start(bf16[4,128,256]{2,1,0:T(8,128)(2,1)S(1)} %collective-permute-done.3.refs_8_.refs_7_), channel_id=1, source_target_pairs={{0,4},{4,0},{8,12},{12,8},{16,20},{20,16},{24,28},{28,24},{32,36},... | collective-permute-start | bytes 786440 | tf_op jit(solution)/shard_map/ppermute | solution.py:365
  24.1 1.2 %copy-start.4 = (bf16[4,128,256]{2,1,0:T(8,128)(2,1)}, bf16[4,128,256]{2,1,0:T(8,128)(2,1)S(1)}, u32[]{:S(2)}) copy-start(bf16[4,128,256]{2,1,0:T(8,128)(2,1)S(1)} %collective-permute-done.6.refs_11_.refs_10_) | copy-start | bytes 786436
  24.3 0.9 copy-start.5
  24.7 0.7 copy-start.6
  25.2 0.7 copy-start.7
  49.9 17.9 %copy-start.26 = (s16[528,256]{1,0:T(8,128)(2,1)S(1)}, s16[528,256]{1,0:T(8,128)(2,1)}, u32[]{:S(2)}) copy-start(s16[528,256]{1,0:T(8,128)(2,1)} %get-tuple-element.57) | copy-start | bytes 811012
  49.9 21.7 %copy-start.25 = (s16[528,256]{1,0:T(8,128)(2,1)S(1)}, s16[528,256]{1,0:T(8,128)(2,1)}, u32[]{:S(2)}) copy-start(s16[528,256]{1,0:T(8,128)(2,1)} %get-tuple-element.58) | copy-start | bytes 811012
  49.9 21.8 %copy-start.24 = (s16[528,256]{1,0:T(8,128)(2,1)S(1)}, s16[528,256]{1,0:T(8,128)(2,1)}, u32[]{:S(2)}) copy-start(s16[528,256]{1,0:T(8,128)(2,1)} %get-tuple-element.59) | copy-start | bytes 811012
  66.7 4.9 %collective-permute-start.16 = (s16[528,256]{1,0:T(8,128)(2,1)}, s16[528,256]{1,0:T(8,128)(2,1)S(1)}, u32[]{:S(2)}, u32[]{:S(2)}) collective-permute-start(s16[528,256]{1,0:T(8,128)(2,1)} %get-tuple-element.60), channel_id=1, source_target_pairs={{0,4},{4,0},{8,12},{12,8},{16,20},{20,16},{24,28},{28,24},{32,36},... | collective-permute-start | bytes 811016 | tf_op jit(solution)/shard_map/ppermute | solution.py:365
  66.8 4.9 %collective-permute-start.17 = (s16[528,256]{1,0:T(8,128)(2,1)}, s16[528,256]{1,0:T(8,128)(2,1)S(1)}, u32[]{:S(2)}, u32[]{:S(2)}) collective-permute-start(s16[528,256]{1,0:T(8,128)(2,1)} %get-tuple-element.61), channel_id=1, source_target_pairs={{0,4},{4,0},{8,12},{12,8},{16,20},{20,16},{24,28},{28,24},{32,36},... | collective-permute-start | bytes 811016 | tf_op jit(solution)/shard_map/ppermute | solution.py:365
  67.3 5.7 %collective-permute-start.18 = (s16[528,256]{1,0:T(8,128)(2,1)}, s16[528,256]{1,0:T(8,128)(2,1)S(1)}, u32[]{:S(2)}, u32[]{:S(2)}) collective-permute-start(s16[528,256]{1,0:T(8,128)(2,1)} %get-tuple-element.62), channel_id=1, source_target_pairs={{0,4},{4,0},{8,12},{12,8},{16,20},{20,16},{24,28},{28,24},{32,36},... | collective-permute-start | bytes 811016 | tf_op jit(solution)/shard_map/ppermute | solution.py:365
  67.4 5.6 %collective-permute-start.19 = (s16[528,256]{1,0:T(8,128)(2,1)}, s16[528,256]{1,0:T(8,128)(2,1)S(1)}, u32[]{:S(2)}, u32[]{:S(2)}) collective-permute-start(s16[528,256]{1,0:T(8,128)(2,1)} %get-tuple-element.63), channel_id=1, source_target_pairs={{0,4},{4,0},{8,12},{12,8},{16,20},{20,16},{24,28},{28,24},{32,36},... | collective-permute-start | bytes 811016 | tf_op jit(solution)/shard_map/ppermute | solution.py:365
  67.8 15.3 %collective-permute-start.10 = (s16[528,256]{1,0:T(8,128)(2,1)S(1)}, s16[528,256]{1,0:T(8,128)(2,1)S(1)}, u32[]{:S(2)}, u32[]{:S(2)}) collective-permute-start(s16[528,256]{1,0:T(8,128)(2,1)S(1)} %copy-done.26), channel_id=1, source_target_pairs={{0,3},{1,0},{2,1},{3,2},{4,7},{5,4},{6,5},{7,6},{8,11},{9,8},{10,9... | collective-permute-start | bytes 811016 | tf_op jit(solution)/shard_map/ppermute | solution.py:348
  71.5 1.4 %copy-start.11 = (s16[528,256]{1,0:T(8,128)(2,1)}, s16[528,256]{1,0:T(8,128)(2,1)S(1)}, u32[]{:S(2)}) copy-start(s16[528,256]{1,0:T(8,128)(2,1)S(1)} %collective-permute-done.16.c0) | copy-start | bytes 811012
  71.6 11.5 %collective-permute-start.11 = (s16[528,256]{1,0:T(8,128)(2,1)S(1)}, s16[528,256]{1,0:T(8,128)(2,1)S(1)}, u32[]{:S(2)}, u32[]{:S(2)}) collective-permute-start(s16[528,256]{1,0:T(8,128)(2,1)S(1)} %copy-done.25), channel_id=1, source_target_pairs={{0,2},{1,3},{2,0},{3,1},{4,6},{5,7},{6,4},{7,5},{8,10},{9,11},{10,... | collective-permute-start | bytes 811016 | tf_op jit(solution)/shard_map/ppermute | solution.py:348
  71.7 1.3 %copy-start.12 = (s16[528,256]{1,0:T(8,128)(2,1)}, s16[528,256]{1,0:T(8,128)(2,1)S(1)}, u32[]{:S(2)}) copy-start(s16[528,256]{1,0:T(8,128)(2,1)S(1)} %collective-permute-done.17.c1) | copy-start | bytes 811012
  71.7 15.3 %collective-permute-start.12 = (s16[528,256]{1,0:T(8,128)(2,1)S(1)}, s16[528,256]{1,0:T(8,128)(2,1)S(1)}, u32[]{:S(2)}, u32[]{:S(2)}) collective-permute-start(s16[528,256]{1,0:T(8,128)(2,1)S(1)} %copy-done.24), channel_id=1, source_target_pairs={{0,1},{1,2},{2,3},{3,0},{4,5},{5,6},{6,7},{7,4},{8,9},{9,10},{10,1... | collective-permute-start | bytes 811016 | tf_op jit(solution)/shard_map/ppermute | solution.py:348
  72.9 0.8 copy-start.14
  77.0 13.3 %collective-permute-start.20 = (s16[528,256]{1,0:T(8,128)(2,1)}, s16[528,256]{1,0:T(8,128)(2,1)S(1)}, u32[]{:S(2)}, u32[]{:S(2)}) collective-permute-start(s16[528,256]{1,0:T(8,128)(2,1)} %get-tuple-element.65), channel_id=1, source_target_pairs={{0,24},{4,100},{8,0},{12,108},{16,8},{20,116},{24,16},{28,124},{32... | collective-permute-start | bytes 811016 | tf_op jit(solution)/shard_map/ppermute | solution.py:362
  77.1 14.4 %collective-permute-start.21 = (s16[528,256]{1,0:T(8,128)(2,1)}, s16[528,256]{1,0:T(8,128)(2,1)S(1)}, u32[]{:S(2)}, u32[]{:S(2)}) collective-permute-start(s16[528,256]{1,0:T(8,128)(2,1)} %get-tuple-element.66), channel_id=1, source_target_pairs={{0,16},{4,68},{8,24},{12,76},{16,0},{20,84},{24,8},{28,92},{32,48}... | collective-permute-start | bytes 811016 | tf_op jit(solution)/shard_map/ppermute | solution.py:362
  83.1 3.9 %copy-start.8 = (s16[528,256]{1,0:T(8,128)(2,1)}, s16[528,256]{1,0:T(8,128)(2,1)S(1)}, u32[]{:S(2)}) copy-start(s16[528,256]{1,0:T(8,128)(2,1)S(1)} %collective-permute-done.10.p1) | copy-start | bytes 811012
  83.1 8.4 %collective-permute-start.22 = (s16[528,256]{1,0:T(8,128)(2,1)}, s16[528,256]{1,0:T(8,128)(2,1)S(1)}, u32[]{:S(2)}, u32[]{:S(2)}) collective-permute-start(s16[528,256]{1,0:T(8,128)(2,1)} %get-tuple-element.67), channel_id=1, source_target_pairs={{0,8},{4,36},{8,16},{12,44},{16,24},{20,52},{24,0},{28,60},{32,40}... | collective-permute-start | bytes 811016 | tf_op jit(solution)/shard_map/ppermute | solution.py:362
  83.1 3.9 %copy-start.9 = (s16[528,256]{1,0:T(8,128)(2,1)}, s16[528,256]{1,0:T(8,128)(2,1)S(1)}, u32[]{:S(2)}) copy-start(s16[528,256]{1,0:T(8,128)(2,1)S(1)} %collective-permute-done.11.p2) | copy-start | bytes 811012
  87.0 0.7 copy-start.10
  90.0 7.6 %collective-permute-start.15 = (s16[528,256]{1,0:T(8,128)(2,1)}, s16[528,256]{1,0:T(8,128)(2,1)S(1)}, u32[]{:S(2)}, u32[]{:S(2)}) collective-permute-start(s16[528,256]{1,0:T(8,128)(2,1)} %user_sum.1.p0), channel_id=1, source_target_pairs={{0,3},{1,0},{2,1},{3,2},{4,7},{5,4},{6,5},{7,6},{8,11},{9,8},{10,9... | collective-permute-start | bytes 811016 | tf_op jit(solution)/shard_map/ppermute | solution.py:348
  90.0 8.3 %collective-permute-start.14 = (s16[528,256]{1,0:T(8,128)(2,1)}, s16[528,256]{1,0:T(8,128)(2,1)S(1)}, u32[]{:S(2)}, u32[]{:S(2)}) collective-permute-start(s16[528,256]{1,0:T(8,128)(2,1)} %user_sum.1.p0), channel_id=1, source_target_pairs={{0,2},{1,3},{2,0},{3,1},{4,6},{5,7},{6,4},{7,5},{8,10},{9,11},{10,... | collective-permute-start | bytes 811016 | tf_op jit(solution)/shard_map/ppermute | solution.py:348
  90.3 1.2 %copy-start.15 = (s16[528,256]{1,0:T(8,128)(2,1)}, s16[528,256]{1,0:T(8,128)(2,1)S(1)}, u32[]{:S(2)}) copy-start(s16[528,256]{1,0:T(8,128)(2,1)S(1)} %collective-permute-done.20.c1) | copy-start | bytes 811012
  90.3 15.5 %collective-permute-start.13 = (s16[528,256]{1,0:T(8,128)(2,1)}, s16[528,256]{1,0:T(8,128)(2,1)S(1)}, u32[]{:S(2)}, u32[]{:S(2)}) collective-permute-start(s16[528,256]{1,0:T(8,128)(2,1)} %user_sum.1.p0), channel_id=1, source_target_pairs={{0,1},{1,2},{2,3},{3,0},{4,5},{5,6},{6,7},{7,4},{8,9},{9,10},{10,1... | collective-permute-start | bytes 811016 | tf_op jit(solution)/shard_map/ppermute | solution.py:348
  91.5 0.7 copy-start.16
  91.5 0.8 copy-start.17
  94.5 14.9 %collective-permute-start.23 = (s16[144,256]{1,0:T(8,128)(2,1)}, s16[144,256]{1,0:T(8,128)(2,1)S(1)}, u32[]{:S(2)}, u32[]{:S(2)}) collective-permute-start(s16[144,256]{1,0:T(8,128)(2,1)} %get-tuple-element.69), channel_id=1, source_target_pairs={{0,96},{4,28},{8,104},{12,4},{16,112},{20,12},{24,120},{28,20},{32... | collective-permute-start | bytes 221192 | tf_op jit(solution)/shard_map/ppermute | solution.py:359
  94.5 14.9 %collective-permute-start.24 = (s16[144,256]{1,0:T(8,128)(2,1)}, s16[144,256]{1,0:T(8,128)(2,1)S(1)}, u32[]{:S(2)}, u32[]{:S(2)}) collective-permute-start(s16[144,256]{1,0:T(8,128)(2,1)} %get-tuple-element.70), channel_id=1, source_target_pairs={{0,64},{4,20},{8,72},{12,28},{16,80},{20,4},{24,88},{28,12},{32,96... | collective-permute-start | bytes 221192 | tf_op jit(solution)/shard_map/ppermute | solution.py:359
  97.5 8.3 %copy-start.18 = (s16[528,256]{1,0:T(8,128)(2,1)}, s16[528,256]{1,0:T(8,128)(2,1)S(1)}, u32[]{:S(2)}) copy-start(s16[528,256]{1,0:T(8,128)(2,1)S(1)} %collective-permute-done.15.p3) | copy-start | bytes 811012
  97.5 11.9 %collective-permute-start.25 = (s16[144,256]{1,0:T(8,128)(2,1)}, s16[144,256]{1,0:T(8,128)(2,1)S(1)}, u32[]{:S(2)}, u32[]{:S(2)}) collective-permute-start(s16[144,256]{1,0:T(8,128)(2,1)} %get-tuple-element.71), channel_id=1, source_target_pairs={{0,32},{4,12},{8,40},{12,20},{16,48},{20,28},{24,56},{28,4},{32,64... | collective-permute-start | bytes 221192 | tf_op jit(solution)/shard_map/ppermute | solution.py:359
  98.3 7.6 %copy-start.19 = (s16[528,256]{1,0:T(8,128)(2,1)}, s16[528,256]{1,0:T(8,128)(2,1)S(1)}, u32[]{:S(2)}) copy-start(s16[528,256]{1,0:T(8,128)(2,1)S(1)} %collective-permute-done.14.p2) | copy-start | bytes 811012
  (5 other events, 3.3 us)
where the time goes:
time: 114 us; the launch traced here: 112 us
  Pallas kernels  55.1 us (48%)
  starting transfers between devices  26.9 us (24%)
  waiting for transfers between devices  22.5 us (20%)
  local copies, waits for them, and re-layouts  4.36 us (4%)
  between operations  1.54 us (1%)
  other arithmetic  1.4 us (1%)
    pallas_call x1, Pallas kernels, local(): pl.pallas_call(user_kernel, out_shape=(f32(quarter, rank),) + (i16(quarte...  23.9 us
    ppermute x6, waiting for transfers between devices, along_y(): lax.ppermute(a, 'items', [(i, (i + k) % items_size) for i in range(items_...  20 us
    pallas_call x1, Pallas kernels, local(): pl.pallas_call(item_kernel, out_shape=(f32(half_rows, rank),) + (i16(part...  16.8 us
    ppermute x8, starting transfers between devices, to_core(): return lax.ppermute(a, 'users', [(i, i ^ 1) for i in spots])  11.2 us
    ppermute x6, starting transfers between devices, along_y(): lax.ppermute(a, 'items', [(i, (i + k) % items_size) for i in range(items_...  6.63 us
    pallas_call x2, Pallas kernels, item_stage(): pl.pallas_call(kernel, out_shape=(f32(size, rank),) + (i16(size + TAIL, r...  5.52 us
    ppermute x6, starting transfers between devices, along_second(): lax.ppermute(a, 'users', [(i, move(i, i % 2 == 1, k)) for i in spots])  5.14 us
    unnamed x54, local copies, waits for them, and re-layouts  4.36 us
  transfers between devices with their start and end apart: 26, of which 9 were waited for; matrix products, arithmetic and copies ran while one was open for 0% of the time, Pallas kernels for 11%

commit v1 on v0

--- a/solution.py
+++ b/solution.py
@@ -11,6 +11,7 @@
 SLOTS = 8
 GROUP = 4
 UNROLL = 2
+TURNS = 8
 RING = 4
 TAIL = 16
 TOP = 32000.0
@@ -99,8 +100,9 @@
     lane = grid(1, 128, 1)
     item_total = jnp.sum(groups, axis=1, keepdims=True)
     numbers = jnp.where(lane == 0, total, item_total).astype(jnp.int32)
-    rounded = (numbers + (UNROLL - 1)) // UNROLL * UNROLL
-    head_ref[...] = jnp.where(lane == 1, here_ref[1], rounded)
+    users_rounded = (numbers + (UNROLL - 1)) // UNROLL * UNROLL
+    items_rounded = (numbers + (TURNS - 1)) // TURNS * TURNS
+    head_ref[...] = jnp.where(lane == 1, here_ref[1], jnp.where(lane == 0, users_rounded, items_rounded))
 
 
 def loads_of(piece_refs, items_ref, sems):
@@ -110,11 +112,11 @@
     ]
 
 
-def user_kernel(*refs):
-    head_ref, pair_ref, tile_ref, panel_ref, factor_ref, users_ref, conf_ref = refs[:7]
-    piece_refs = refs[7:15]
-    user_own, user_1, user_2, user_3, weight_out = refs[15:20]
-    items_ref, user_acc, conf_buf, weights_ref, sems, piece_sems, out_sems = refs[20:]
+def tile_kernel(*refs):
+    head_ref, pair_ref, tile_ref, panel_ref, factor_ref, group_ref, spot_ref, block_ref, users_ref, conf_ref = refs[:10]
+    piece_refs = refs[10:18]
+    user_own, user_1, user_2, user_3, item_own, item_code = refs[18:24]
+    items_ref, user_acc, item_acc, conf_buf, weights_ref, sems, piece_sems = refs[24:]
     edge = conf_buf.shape[2]
     rank = users_ref.shape[1]
     groups = head_ref[0, 0]
@@ -134,13 +136,12 @@
         slot = lax.rem(p, SLOTS)
         pltpu.make_async_copy(conf_ref.at[pl.ds(0, GROUP)], conf_buf.at[slot], sems.at[slot]).wait()
 
-    def leave(p):
-        rows = pl.ds(GROUP * p, GROUP)
-        return pltpu.make_async_copy(weights_ref.at[rows], weight_out.at[rows], out_sems.at[p])
-
     for s in range(SLOTS):
         fetch(s)
 
+    user_gram = dot(users_ref[...], users_ref[...], 0, 0)
+    user_high, user_low = split(GRAM_WEIGHT * user_gram)
+    item_acc[...] = jnp.zeros(item_acc.shape, jnp.float32)
     item_gram = jnp.zeros((rank, rank), jnp.float32)
     for i, c in enumerate(loads):
         c.wait()
@@ -179,7 +180,6 @@
             arrive(base + UNROLL + j)
         for j in range(UNROLL):
             fetch(base + j + SLOTS)
-            leave(base + j).start()
         terms = []
         for j in range(UNROLL):
             g = base + j
@@ -195,104 +195,65 @@
         return carry
 
     lax.fori_loop(0, groups // UNROLL, visit, 0)
-    for j in range(UNROLL):
-        leave(groups + j).start()
     for j in range(UNROLL, SLOTS):
         arrive(groups + j)
-    user_own[...] = user_acc[:quarter, :]
-    for k, out in enumerate((user_1, user_2, user_3)):
-        encode(out, user_acc[(k + 1) * quarter:(k + 2) * quarter, :])
-
-    def drain(p, carry):
-        leave(p).wait()
-        return carry
-
-    lax.fori_loop(0, groups + UNROLL, drain, 0)
-
-
-def item_kernel(*refs):
-    head_ref, group_ref, spot_ref, block_ref, users_ref, weight_ref = refs[:6]
-    piece_refs = refs[6:14]
-    item_own, item_0, item_1, item_2, item_3 = refs[14:19]
-    items_ref, item_acc, buf, sems, piece_sems = refs[19:]
-    edge = buf.shape[2]
-    rank = users_ref.shape[1]
-    groups = head_ref[0, 2]
-
-    loads = loads_of(piece_refs, items_ref, piece_sems)
-    for c in loads:
-        c.start()
-
-    def fetch(p):
-        slot = lax.rem(p, SLOTS)
-        for k in range(GROUP):
-            spot = spot_ref[0, GROUP * p + k]
-            pltpu.make_async_copy(weight_ref.at[spot], buf.at[slot, k], sems.at[slot]).start()
-
-    def arrive(p):
-        slot = lax.rem(p, SLOTS)
-        pltpu.make_async_copy(weight_ref.at[pl.ds(0, GROUP)], buf.at[slot], sems.at[slot]).wait()
-
-    ahead = SLOTS - UNROLL
-    for s in range(ahead):
-        fetch(s)
-
-    item_acc[...] = jnp.zeros(item_acc.shape, jnp.float32)
-    user_gram = dot(users_ref[...], users_ref[...], 0, 0)
-    high, low = split(GRAM_WEIGHT * user_gram)
-
-    def visit(i, carry):
-        base = i * UNROLL
-        for j in range(UNROLL):
-            arrive(base + j)
-        for j in range(UNROLL):
-            fetch(base + j + ahead)
-
+
+    def turn(i, carry):
+        base = i * TURNS
         terms = []
-        for j in range(UNROLL):
+        for j in range(TURNS):
             g = base + j
             parts = []
             for k in range(GROUP):
                 u = pl.multiple_of(block_ref[0, GROUP * g + k] * edge, edge)
                 parts.append(users_ref[pl.ds(u, edge), :])
-            weights = buf[lax.rem(g, SLOTS)].reshape(GROUP * edge, edge)
+            weights = jnp.concatenate([weights_ref[spot_ref[0, GROUP * g + k]] for k in range(GROUP)], axis=0)
             terms.append(dot(weights, jnp.concatenate(parts, axis=0), 0, 0))
-        for j in range(UNROLL):
+        for j in range(TURNS):
             r = pl.multiple_of(group_ref[0, base + j] * edge, edge)
             item_acc[pl.ds(r, edge), :] += terms[j]
         return carry
 
-    lax.fori_loop(0, groups // UNROLL, visit, 0)
-    for j in range(ahead):
-        arrive(groups + j)
-    for c in loads:
-        c.wait()
-    part = item_0.shape[0] - TAIL
-    for k, out in enumerate((None, None, None, None, item_0, item_1, item_2, item_3)):
+    lax.fori_loop(0, head_ref[0, 2] // TURNS, turn, 0)
+    user_own[...] = user_acc[:quarter, :]
+    for k, out in enumerate((user_1, user_2, user_3)):
+        encode(out, user_acc[(k + 1) * quarter:(k + 2) * quarter, :])
+    part = item_acc.shape[0] // 8
+    for k in range(8):
         items = items_ref[RING * k:RING * (k + 1)].reshape(part, rank)
-        total = item_acc[k * part:(k + 1) * part, :] + (dot(items, high, 1, 0) + dot(items, low, 1, 0))
-        if out is None:
+        total = item_acc[k * part:(k + 1) * part, :] + (dot(items, user_high, 1, 0) + dot(items, user_low, 1, 0))
+        if k < RING:
             item_own[k * part:(k + 1) * part, :] = total
         else:
+            encode(item_code.at[pl.ds((k - RING) * (part + TAIL), part + TAIL)], total)
+
+
+def user_sum_kernel(own_ref, p1, p2, p3, out_ref):
+    encode(out_ref, (own_ref[...] + decode(p1)) + (decode(p2) + decode(p3)))
+
+
+def final_kernel(here_ref, p0, p1, p2, p3, own_ref, q1, q2, q3, user_out, item_out, buf, sems):
+    quarter = p0.shape[0] - TAIL
+    copies = []
+    for k, p in enumerate((p0, p1, p2, p3)):
+        buf[k] = GRAD_SCALE * decode(p)
+        q = pl.multiple_of(((here_ref[1] - k) & 3) * quarter, quarter)
+        copies.append(pltpu.make_async_copy(buf.at[k], user_out.at[pl.ds(q, quarter)], sems.at[k]))
+        copies[-1].start()
+    item_out[...] = GRAD_SCALE * ((own_ref[...] + decode(q1)) + (decode(q2) + decode(q3)))
+    for c in copies:
+        c.wait()
+
+
+def item_core_kernel(own_ref, code_ref, own_out, p1, p2, p3):
+    part = own_out.shape[0]
+    for k, out in enumerate((own_out, p1, p2, p3)):
+        code = code_ref.at[pl.ds(k * (part + TAIL), part + TAIL)]
+        total = own_ref[k * part:(k + 1) * part, :] + decode(code)
+        if k == 0:
+            out[...] = total
+        else:
             encode(out, total)
-
-
-def user_sum_kernel(after_ref, own_ref, p1, p2, p3, out_ref):
-    encode(out_ref, (own_ref[...] + decode(p1)) + (decode(p2) + decode(p3)))
-
-
-def user_out_kernel(here_ref, p0, p1, p2, p3, out_ref):
-    quarter = p0.shape[0] - TAIL
-    for k, p in enumerate((p0, p1, p2, p3)):
-        q = pl.multiple_of(((here_ref[1] - k) & 3) * quarter, quarter)
-        out_ref[pl.ds(q, quarter), :] = GRAD_SCALE * decode(p)
-
-
-def item_core_kernel(own_ref, c0, c1, c2, c3, own_out, p1, p2, p3):
-    part = own_out.shape[0]
-    own_out[...] = own_ref[:part, :] + decode(c0)
-    for k, (c, out) in enumerate(((c1, p1), (c2, p2), (c3, p3))):
-        encode(out, own_ref[(k + 1) * part:(k + 2) * part, :] + decode(c))
 
 
 def item_mid_kernel(own_ref, c1, c2, c3, own_out, p1, p2, p3):
@@ -303,10 +264,6 @@
         encode(out, total[(k + 1) * part:(k + 2) * part])
 
 
-def item_out_kernel(own_ref, p1, p2, p3, out_ref):
-    out_ref[...] = GRAD_SCALE * ((own_ref[...] + decode(p1)) + (decode(p2) + decode(p3)))
-
-
 def smem():
     return pl.BlockSpec(memory_space=pltpu.SMEM)
 
@@ -325,10 +282,6 @@
 
 def i32(*shape):
     return jax.ShapeDtypeStruct(shape, jnp.int32)
-
-
-def bf16(*shape):
-    return jax.ShapeDtypeStruct(shape, jnp.bfloat16)
 
 
 def i16(*shape):
@@ -369,7 +322,7 @@
 
     own = item_factors[0]
     first = [own] + [along_first(own, k) for k in (1, 2, 3)]
-    spot_total = -(-(max(GROUP * pairs, tiles + (GROUP - 1) * users_size) + GROUP * (SLOTS + UNROLL)) // 128) * 128
+    spot_total = -(-(max(GROUP * pairs, tiles + (GROUP - 1) * users_size) + GROUP * (SLOTS + UNROLL + TURNS)) // 128) * 128
     plan = pl.pallas_call(
         plan_kernel,
         out_shape=(i32(1, 128), i32(1, 128), i32(1, spot_total), i32(1, spot_total), f32(1, spot_total), i32(1, 128), i32(1, spot_total), i32(1, spot_total)),
@@ -386,50 +339,35 @@
     panels = users_size
     half_rows = panels * edge // 2
     part = half_rows // 4
-    head, pair, tile, panel, factor, group, spot, block = plan
-    *user_parts, weights = pl.pallas_call(
-        user_kernel,
-        out_shape=(f32(quarter, rank),) + (i16(quarter + TAIL, rank),) * 3 + (bf16(GROUP * pairs, edge, edge),),
-        in_specs=[smem()] * 5 + [vmem(), anywhere()] + [anywhere()] * 8,
-        out_specs=[vmem()] * 4 + [anywhere()],
+    user_own, *user_parts, item_own, item_code = pl.pallas_call(
+        tile_kernel,
+        out_shape=(f32(quarter, rank),)
+        + (i16(quarter + TAIL, rank),) * 3
+        + (f32(half_rows, rank), i16(4 * (part + TAIL), rank)),
+        in_specs=[smem()] * 8 + [vmem(), anywhere()] + [anywhere()] * 8,
+        out_specs=[vmem()] * 6,
         scratch_shapes=[
             pltpu.VMEM((panels, edge, rank), jnp.bfloat16),
             pltpu.VMEM((rows, rank), jnp.float32),
+            pltpu.VMEM((panels * edge, rank), jnp.float32),
             pltpu.VMEM((SLOTS, GROUP, edge, edge), jnp.bfloat16),
             pltpu.VMEM((GROUP * pairs, edge, edge), jnp.bfloat16),
             pltpu.SemaphoreType.DMA((SLOTS,)),
             pltpu.SemaphoreType.DMA((8,)),
-            pltpu.SemaphoreType.DMA((pairs,)),
         ],
-        name="tiles_user",
-    )(head, pair, tile, panel, factor, user_factors, confidence[0, 0], *pieces)
-    item_own, *item_parts = pl.pallas_call(
-        item_kernel,
-        out_shape=(f32(half_rows, rank),) + (i16(part + TAIL, rank),) * 4,
-        in_specs=[smem()] * 4 + [vmem(), anywhere()] + [anywhere()] * 8,
-        out_specs=[vmem()] * 5,
-        scratch_shapes=[
-            pltpu.VMEM((panels, edge, rank), jnp.bfloat16),
-            pltpu.VMEM((panels * edge, rank), jnp.float32),
-            pltpu.VMEM((SLOTS, GROUP, edge, edge), jnp.bfloat16),
-            pltpu.SemaphoreType.DMA((SLOTS,)),
-            pltpu.SemaphoreType.DMA((8,)),
-        ],
-        name="tiles_item",
-    )(head, group, spot, block, user_factors, weights, *pieces)
-    user_own, *user_parts = user_parts
-    after = item_own
-
-    item_parts = [to_core(a) for a in item_parts]
+        name="tiles",
+    )(*plan, user_factors, confidence[0, 0], *pieces)
+
+    item_code = to_core(item_code)
     user_parts = [along_y(a, -k) for k, a in zip((1, 2, 3), user_parts)]
 
     user_code = pl.pallas_call(
         user_sum_kernel,
         out_shape=i16(quarter + TAIL, rank),
-        in_specs=[anywhere()] + [vmem()] * 4,
+        in_specs=[vmem()] * 4,
         out_specs=vmem(),
         name="user_sum",
-    )(after, user_own, *user_parts)
+    )(user_own, *user_parts)
 
     def item_stage(kernel, size, *ins):
         return pl.pallas_call(
@@ -439,25 +377,19 @@
             out_specs=[vmem()] * 4,
         )(*ins)
 
-    item_own, *item_parts = item_stage(item_core_kernel, part, item_own, *item_parts)
+    item_own, *item_parts = item_stage(item_core_kernel, part, item_own, item_code)
     item_parts = [along_second(a, -k) for k, a in zip((1, 2, 3), item_parts)]
     user_codes = [user_code] + [along_y(user_code, k) for k in (1, 2, 3)]
     item_own, *item_parts = item_stage(item_mid_kernel, edge, item_own, *item_parts)
     item_parts = [along_first(a, -k) for k, a in zip((1, 2, 3), item_parts)]
-    item_grad = pl.pallas_call(
-        item_out_kernel,
-        out_shape=f32(edge, rank),
-        in_specs=[vmem()] * 4,
-        out_specs=vmem(),
-        name="item_out",
-    )(item_own, *item_parts)
-    user_grad = pl.pallas_call(
-        user_out_kernel,
-        out_shape=f32(rows, rank),
-        in_specs=[smem()] + [vmem()] * 4,
-        out_specs=vmem(),
-        name="user_out",
-    )(here, *user_codes)
+    user_grad, item_grad = pl.pallas_call(
+        final_kernel,
+        out_shape=(f32(rows, rank), f32(edge, rank)),
+        in_specs=[smem()] + [vmem()] * 8,
+        out_specs=[anywhere(), vmem()],
+        scratch_shapes=[pltpu.VMEM((4, quarter, rank), jnp.float32), pltpu.SemaphoreType.DMA((4,))],
+        name="final",
+    )(here, *user_codes, item_own, *item_parts)
     return user_grad, item_grad[None]
 
 

time: 114 us -> 98.9 us (0.87)
  the two profiles are of different devices: /device:TPU:7 before, /device:TPU:0 now
where the time goes in v1:
time: 98.9 us; the launch traced here: 97.8 us
  starting transfers between devices  33.4 us (34%)
  Pallas kernels  31.2 us (32%)
  waiting for transfers between devices  26.3 us (27%)
  local copies, waits for them, and re-layouts  3.85 us (4%)
  between operations  1.64 us (2%)
  other arithmetic  1.39 us (1%)
    pallas_call x1, Pallas kernels, local(): pl.pallas_call(tile_kernel, out_shape=(f32(quarter, rank),) + (i16(quarte...  17.9 us
    ppermute x6, waiting for transfers between devices, along_y(): lax.ppermute(a, 'items', [(i, (i + k) % items_size) for i in range(items_...  13.1 us
    ppermute x6, starting transfers between devices, along_y(): lax.ppermute(a, 'items', [(i, (i + k) % items_size) for i in range(items_...  10.3 us
    ppermute x6, starting transfers between devices, along_first(): lax.ppermute(a, 'users', [(i, move(i, i % 2 == 0, k)) for i in spots])  9.52 us
    ppermute x6, waiting for transfers between devices, along_second(): lax.ppermute(a, 'users', [(i, move(i, i % 2 == 1, k)) for i in spots])  8.99 us
    ppermute x6, starting transfers between devices, along_second(): lax.ppermute(a, 'users', [(i, move(i, i % 2 == 1, k)) for i in spots])  6.8 us
    ppermute x5, starting transfers between devices, to_core(): return lax.ppermute(a, 'users', [(i, i ^ 1) for i in spots])  6.78 us
    pallas_call x2, Pallas kernels, item_stage(): pl.pallas_call(kernel, out_shape=(f32(size, rank),) + (i16(size + TAIL, r...  5.52 us
  transfers between devices with their start and end apart: 23, of which 12 were waited for; matrix products, arithmetic and copies ran while one was open for 1% of the time, Pallas kernels for 10%

profile of v1, /device:TPU:0, one launch (start us, length us, event | category | flops | bytes accessed | tf_op | source)
XLA Modules:
  0.0 97.8 jit_solution(6184954903395325398)
XLA Ops:
  0.6 4.2 %collective-permute-start.2 = (bf16[128,256]{1,0:T(8,128)(2,1)}, bf16[128,256]{1,0:T(8,128)(2,1)S(1)}, u32[]{:S(2)}, u32[]{:S(2)}) collective-permute-start(bf16[128,256]{1,0:T(8,128)(2,1)} %bitcast.12), channel_id=1, source_target_pairs={{0,96},{4,28},{8,104},{12,4},{16,112},{20,12},{24,120},{28,20},{32... | collective-permute-start | bytes 196616 | tf_op jit(solution)/shard_map/ppermute | solution.py:312
  4.8 1.3 %collective-permute-start = (bf16[128,256]{1,0:T(8,128)(2,1)}, bf16[128,256]{1,0:T(8,128)(2,1)S(1)}, u32[]{:S(2)}, u32[]{:S(2)}) collective-permute-start(bf16[128,256]{1,0:T(8,128)(2,1)} %bitcast.14), channel_id=1, source_target_pairs={{0,32},{4,12},{8,40},{12,20},{16,48},{20,28},{24,56},{28,4},{32,64... | collective-permute-start | bytes 196616 | tf_op jit(solution)/shard_map/ppermute | solution.py:312
  6.8 0.5 compare_select_fusion.here_ref
  7.3 2.1 %plan.1 = (s32[1,128]{1,0:T(1,128)}, s32[1,128]{1,0:T(1,128)}, s32[1,512]{1,0:T(1,128)}, s32[1,512]{1,0:T(1,128)}, f32[1,512]{1,0:T(1,128)}, /*index=5*/s32[1,12...) custom-call(s32[2]{0:T(128)} %compare_select_fusion.here_ref, s32[1]{0:T(128)} %bitcast.10.live_ref, s32[1,256]{1,0:T(1,128)} %bitcast.18, ...), custom_call_target="tpu_custom_call" | custom-call | tf_op jit(solution)/shard_map/plan/pallas_call | solution.py:326
  9.4 1.5 %collective-permute-done.1 = bf16[128,256]{1,0:T(8,128)(2,1)S(1)} collective-permute-done((bf16[128,256]{1,0:T(8,128)(2,1)}, bf16[128,256]{1,0:T(8,128)(2,1)S(1)}, u32[]{:S(2)}, u32[]{:S(2)}) %collective-permute-start.1) | collective-permute-done | bytes 65568 | tf_op jit(solution)/shard_map/ppermute | solution.py:312
  10.9 0.3 collective-permute-done
  11.2 0.9 pad_maximum_fusion.refs_10_
  12.1 2.8 %collective-permute-start.5 = (bf16[4,128,256]{2,1,0:T(8,128)(2,1)S(1)}, bf16[4,128,256]{2,1,0:T(8,128)(2,1)S(1)}, u32[]{:S(2)}, u32[]{:S(2)}) collective-permute-start(bf16[4,128,256]{2,1,0:T(8,128)(2,1)S(1)} %pad_maximum_fusion.refs_10_), channel_id=1, source_target_pairs={{0,24},{4,100},{8,0},{12,108},{16,8},{20,116},{24,16},{28,124},{32... | collective-permute-start | bytes 786440 | tf_op jit(solution)/shard_map/ppermute | solution.py:315
  15.0 0.8 collective-permute-start.4
  15.8 0.9 collective-permute-start.3
  16.6 0.0 collective-permute-start.6
  16.6 5.0 %collective-permute-done.5.refs_13_ = bf16[4,128,256]{2,1,0:T(8,128)(2,1)S(1)} collective-permute-done((bf16[4,128,256]{2,1,0:T(8,128)(2,1)S(1)}, bf16[4,128,256]{2,1,0:T(8,128)(2,1)S(1)}, u32[]{:S(2)}, u32[]{:S(2)}) %collective-permute-start.5) | collective-permute-done | bytes 262176 | tf_op jit(solution)/shard_map/ppermute | solution.py:315
  21.7 0.0 collective-permute-start.9
  21.7 1.2 %collective-permute-done.4.refs_12_ = bf16[4,128,256]{2,1,0:T(8,128)(2,1)S(1)} collective-permute-done((bf16[4,128,256]{2,1,0:T(8,128)(2,1)S(1)}, bf16[4,128,256]{2,1,0:T(8,128)(2,1)S(1)}, u32[]{:S(2)}, u32[]{:S(2)}) %collective-permute-start.4) | collective-permute-done | bytes 262176 | tf_op jit(solution)/shard_map/ppermute | solution.py:315
  22.9 0.0 collective-permute-start.8
  22.9 2.7 %collective-permute-done.3.refs_11_ = bf16[4,128,256]{2,1,0:T(8,128)(2,1)S(1)} collective-permute-done((bf16[4,128,256]{2,1,0:T(8,128)(2,1)S(1)}, bf16[4,128,256]{2,1,0:T(8,128)(2,1)S(1)}, u32[]{:S(2)}, u32[]{:S(2)}) %collective-permute-start.3) | collective-permute-done | bytes 262176 | tf_op jit(solution)/shard_map/ppermute | solution.py:315
  25.6 0.0 collective-permute-start.7
  25.7 1.5 %collective-permute-done.7.refs_15_ = bf16[4,128,256]{2,1,0:T(8,128)(2,1)S(1)} collective-permute-done((bf16[4,128,256]{2,1,0:T(8,128)(2,1)S(1)}, bf16[4,128,256]{2,1,0:T(8,128)(2,1)S(1)}, u32[]{:S(2)}, u32[]{:S(2)}) %collective-permute-start.7) | collective-permute-done | bytes 262176 | tf_op jit(solution)/shard_map/ppermute | solution.py:318
  27.2 0.7 copy-done.17
  27.9 17.9 %tiles.1 = (f32[512,256]{1,0:T(8,128)}, s16[528,256]{1,0:T(8,128)(2,1)}, s16[528,256]{1,0:T(8,128)(2,1)}, s16[528,256]{1,0:T(8,128)(2,1)}, f32[2048,256]{1,0:T(8,128)}, /*index=5*/s16[2112,256]{1,0:T(8,128)(2,1)}) custom-call(s32[1,128]{1,0:T(1,128)} %get-tuple-element.43.refs_0_, s32[1,128]{1,0:T(1,128)} %get-tuple-element.44.refs_1_, ...), custom_call_target="tpu_custom_call" | custom-call | tf_op jit(solution)/shard_map/tiles/pallas_call | solution.py:342
  45.8 6.8 %collective-permute-start.16 = (s16[2112,256]{1,0:T(8,128)(2,1)}, s16[2112,256]{1,0:T(8,128)(2,1)S(1)}, u32[]{:S(2)}, u32[]{:S(2)}) collective-permute-start(s16[2112,256]{1,0:T(8,128)(2,1)} %get-tuple-element.57), channel_id=1, source_target_pairs={{0,4},{4,0},{8,12},{12,8},{16,20},{20,16},{24,28},{28,24},{32,36},... | collective-permute-start | bytes 3244040 | tf_op jit(solution)/shard_map/ppermute | solution.py:318
  52.5 5.2 %collective-permute-start.10 = (s16[528,256]{1,0:T(8,128)(2,1)}, s16[528,256]{1,0:T(8,128)(2,1)S(1)}, u32[]{:S(2)}, u32[]{:S(2)}) collective-permute-start(s16[528,256]{1,0:T(8,128)(2,1)} %get-tuple-element.53), channel_id=1, source_target_pairs={{0,3},{1,0},{2,1},{3,2},{4,7},{5,4},{6,5},{7,6},{8,11},{9,8},{10,9... | collective-permute-start | bytes 811016 | tf_op jit(solution)/shard_map/ppermute | solution.py:301
  57.7 1.1 %collective-permute-start.11 = (s16[528,256]{1,0:T(8,128)(2,1)}, s16[528,256]{1,0:T(8,128)(2,1)S(1)}, u32[]{:S(2)}, u32[]{:S(2)}) collective-permute-start(s16[528,256]{1,0:T(8,128)(2,1)} %get-tuple-element.54), channel_id=1, source_target_pairs={{0,2},{1,3},{2,0},{3,1},{4,6},{5,7},{6,4},{7,5},{8,10},{9,11},{10,... | collective-permute-start | bytes 811016 | tf_op jit(solution)/shard_map/ppermute | solution.py:301
  58.8 1.3 %collective-permute-start.12 = (s16[528,256]{1,0:T(8,128)(2,1)}, s16[528,256]{1,0:T(8,128)(2,1)S(1)}, u32[]{:S(2)}, u32[]{:S(2)}) collective-permute-start(s16[528,256]{1,0:T(8,128)(2,1)} %get-tuple-element.55), channel_id=1, source_target_pairs={{0,1},{1,2},{2,3},{3,0},{4,5},{5,6},{6,7},{7,4},{8,9},{9,10},{10,1... | collective-permute-start | bytes 811016 | tf_op jit(solution)/shard_map/ppermute | solution.py:301
  60.1 1.0 %copy-done = s16[2112,256]{1,0:T(8,128)(2,1)} copy-done((s16[2112,256]{1,0:T(8,128)(2,1)}, s16[2112,256]{1,0:T(8,128)(2,1)S(1)}, u32[]{:S(2)}) %copy-start) | copy-done | bytes 1081368
  61.1 3.3 %shard_map.95 = (f32[512,256]{1,0:T(8,128)}, s16[528,256]{1,0:T(8,128)(2,1)}, s16[528,256]{1,0:T(8,128)(2,1)}, s16[528,256]{1,0:T(8,128)(2,1)}) custom-call(f32[2048,256]{1,0:T(8,128)} %get-tuple-element.56.own_ref, s16[2112,256]{1,0:T(8,128)(2,1)} %copy-done), custom_call_target="tpu_custom_call" | custom-call | tf_op jit(solution)/shard_map/pallas_call | solution.py:373
  64.5 2.1 %collective-permute-start.17 = (s16[528,256]{1,0:T(8,128)(2,1)}, s16[528,256]{1,0:T(8,128)(2,1)S(1)}, u32[]{:S(2)}, u32[]{:S(2)}) collective-permute-start(s16[528,256]{1,0:T(8,128)(2,1)} %get-tuple-element.59), channel_id=1, source_target_pairs={{0,24},{4,100},{8,0},{12,108},{16,8},{20,116},{24,16},{28,124},{32... | collective-permute-start | bytes 811016 | tf_op jit(solution)/shard_map/ppermute | solution.py:315
  66.5 0.2 collective-permute-start.18
  66.7 3.4 %collective-permute-done.10.p1 = s16[528,256]{1,0:T(8,128)(2,1)S(1)} collective-permute-done((s16[528,256]{1,0:T(8,128)(2,1)}, s16[528,256]{1,0:T(8,128)(2,1)S(1)}, u32[]{:S(2)}, u32[]{:S(2)}) %collective-permute-start.10) | collective-permute-done | bytes 270368 | tf_op jit(solution)/shard_map/ppermute | solution.py:301
  70.1 0.0 collective-permute-start.19
  70.2 3.6 %collective-permute-done.12.p3 = s16[528,256]{1,0:T(8,128)(2,1)S(1)} collective-permute-done((s16[528,256]{1,0:T(8,128)(2,1)}, s16[528,256]{1,0:T(8,128)(2,1)S(1)}, u32[]{:S(2)}, u32[]{:S(2)}) %collective-permute-start.12) | collective-permute-done | bytes 270368 | tf_op jit(solution)/shard_map/ppermute | solution.py:301
  73.7 0.7 copy-done.4
  74.5 2.3 %user_sum.1.p0 = s16[528,256]{1,0:T(8,128)(2,1)} custom-call(f32[512,256]{1,0:T(8,128)} %get-tuple-element.52.own_ref, s16[528,256]{1,0:T(8,128)(2,1)} %copy-done.2, s16[528,256]{1,0:T(8,128)(2,1)} %copy-done.3, s16[528,256]{1,0:T(8,128)(2,1)} %copy-done.4), custom_call_target="tpu_custom_call" | custom-call | tf_op jit(solution)/shard_map/user_sum/pallas_call | solution.py:364
  76.7 0.6 collective-permute-start.15
  77.3 1.3 %collective-permute-start.14 = (s16[528,256]{1,0:T(8,128)(2,1)}, s16[528,256]{1,0:T(8,128)(2,1)S(1)}, u32[]{:S(2)}, u32[]{:S(2)}) collective-permute-start(s16[528,256]{1,0:T(8,128)(2,1)} %user_sum.1.p0), channel_id=1, source_target_pairs={{0,2},{1,3},{2,0},{3,1},{4,6},{5,7},{6,4},{7,5},{8,10},{9,11},{10,... | collective-permute-start | bytes 811016 | tf_op jit(solution)/shard_map/ppermute | solution.py:301
  78.7 0.8 collective-permute-start.13
  79.5 0.7 copy-done.9
  80.2 0.1 copy-done.10
  80.3 2.2 %shard_map.96 = (f32[128,256]{1,0:T(8,128)}, s16[144,256]{1,0:T(8,128)(2,1)}, s16[144,256]{1,0:T(8,128)(2,1)}, s16[144,256]{1,0:T(8,128)(2,1)}) custom-call(f32[512,256]{1,0:T(8,128)} %get-tuple-element.58.own_ref, s16[528,256]{1,0:T(8,128)(2,1)} %copy-done.8, s16[528,256]{1,0:T(8,128)(2,1)} %copy-done.9, s16[528,256]{1,0:T(8,128)(2,1)} %copy-done.10), custom_call_target="tpu_custom_call" | custom-call | tf_op jit(solution)/shard_map/pallas_call | solution.py:373
  82.5 0.1 collective-permute-start.20
  82.6 3.6 %collective-permute-start.21 = (s16[144,256]{1,0:T(8,128)(2,1)}, s16[144,256]{1,0:T(8,128)(2,1)S(1)}, u32[]{:S(2)}, u32[]{:S(2)}) collective-permute-start(s16[144,256]{1,0:T(8,128)(2,1)} %get-tuple-element.64), channel_id=1, source_target_pairs={{0,64},{4,20},{8,72},{12,28},{16,80},{20,4},{24,88},{28,12},{32,96... | collective-permute-start | bytes 221192 | tf_op jit(solution)/shard_map/ppermute | solution.py:312
  86.2 0.1 collective-permute-done.15.p3
  86.3 0.4 collective-permute-start.22
  86.7 1.8 %collective-permute-done.14.p2 = s16[528,256]{1,0:T(8,128)(2,1)S(1)} collective-permute-done((s16[528,256]{1,0:T(8,128)(2,1)}, s16[528,256]{1,0:T(8,128)(2,1)S(1)}, u32[]{:S(2)}, u32[]{:S(2)}) %collective-permute-start.14) | collective-permute-done | bytes 270368 | tf_op jit(solution)/shard_map/ppermute | solution.py:301
  88.5 4.2 %collective-permute-done.13.p1 = s16[528,256]{1,0:T(8,128)(2,1)S(1)} collective-permute-done((s16[528,256]{1,0:T(8,128)(2,1)}, s16[528,256]{1,0:T(8,128)(2,1)S(1)}, u32[]{:S(2)}, u32[]{:S(2)}) %collective-permute-start.13) | collective-permute-done | bytes 270368 | tf_op jit(solution)/shard_map/ppermute | solution.py:301
  92.7 1.0 collective-permute-done.22.q3
  93.7 0.6 copy-done.20
  94.3 3.4 %final.1 = (f32[2048,256]{1,0:T(8,128)}, f32[128,256]{1,0:T(8,128)}) custom-call(s32[2]{0:T(128)} %compare_select_fusion.here_ref, s16[528,256]{1,0:T(8,128)(2,1)} %user_sum.1.p0, s16[528,256]{1,0:T(8,128)(2,1)} %copy-done.7, s16[528,256]{1,0:T(8,128)(2,1)} %copy-done.6, s16[528,256]{1,0:T(8,128)(2,1)} %copy-done.5, f32[128,256]{1,0:T(8,128)} %get-tuple-element.62.own_ref, ...), custom_call_target="tpu_custom_call" | custom-call | tf_op jit(solution)/shard_map/final/pallas_call | solution.py:385
  (48 shorter events, 0.1 us)
Async XLA Ops:
  0.6 8.8 %collective-permute-start.2 = (bf16[128,256]{1,0:T(8,128)(2,1)}, bf16[128,256]{1,0:T(8,128)(2,1)S(1)}, u32[]{:S(2)}, u32[]{:S(2)}) collective-permute-start(bf16[128,256]{1,0:T(8,128)(2,1)} %bitcast.12), channel_id=1, source_target_pairs={{0,96},{4,28},{8,104},{12,4},{16,112},{20,12},{24,120},{28,20},{32... | collective-permute-start | bytes 196616 | tf_op jit(solution)/shard_map/ppermute | solution.py:312
  4.8 6.1 %collective-permute-start.1 = (bf16[128,256]{1,0:T(8,128)(2,1)}, bf16[128,256]{1,0:T(8,128)(2,1)S(1)}, u32[]{:S(2)}, u32[]{:S(2)}) collective-permute-start(bf16[128,256]{1,0:T(8,128)(2,1)} %bitcast.13), channel_id=1, source_target_pairs={{0,64},{4,20},{8,72},{12,28},{16,80},{20,4},{24,88},{28,12},{32,96... | collective-permute-start | bytes 196616 | tf_op jit(solution)/shard_map/ppermute | solution.py:312
  4.8 6.4 %collective-permute-start = (bf16[128,256]{1,0:T(8,128)(2,1)}, bf16[128,256]{1,0:T(8,128)(2,1)S(1)}, u32[]{:S(2)}, u32[]{:S(2)}) collective-permute-start(bf16[128,256]{1,0:T(8,128)(2,1)} %bitcast.14), channel_id=1, source_target_pairs={{0,32},{4,12},{8,40},{12,20},{16,48},{20,28},{24,56},{28,4},{32,64... | collective-permute-start | bytes 196616 | tf_op jit(solution)/shard_map/ppermute | solution.py:312
  12.1 15.1 %copy-start.1 = (bf16[4,128,256]{2,1,0:T(8,128)(2,1)}, bf16[4,128,256]{2,1,0:T(8,128)(2,1)S(1)}, u32[]{:S(2)}) copy-start(bf16[4,128,256]{2,1,0:T(8,128)(2,1)S(1)} %pad_maximum_fusion.refs_10_) | copy-start | bytes 786436
  12.1 9.6 %collective-permute-start.5 = (bf16[4,128,256]{2,1,0:T(8,128)(2,1)S(1)}, bf16[4,128,256]{2,1,0:T(8,128)(2,1)S(1)}, u32[]{:S(2)}, u32[]{:S(2)}) collective-permute-start(bf16[4,128,256]{2,1,0:T(8,128)(2,1)S(1)} %pad_maximum_fusion.refs_10_), channel_id=1, source_target_pairs={{0,24},{4,100},{8,0},{12,108},{16,8},{20,116},{24,16},{28,124},{32... | collective-permute-start | bytes 786440 | tf_op jit(solution)/shard_map/ppermute | solution.py:315
  15.0 8.0 %collective-permute-start.4 = (bf16[4,128,256]{2,1,0:T(8,128)(2,1)S(1)}, bf16[4,128,256]{2,1,0:T(8,128)(2,1)S(1)}, u32[]{:S(2)}, u32[]{:S(2)}) collective-permute-start(bf16[4,128,256]{2,1,0:T(8,128)(2,1)S(1)} %pad_maximum_fusion.refs_10_), channel_id=1, source_target_pairs={{0,16},{4,68},{8,24},{12,76},{16,0},{20,84},{24,8},{28,92},{32,48}... | collective-permute-start | bytes 786440 | tf_op jit(solution)/shard_map/ppermute | solution.py:315
  15.8 9.9 %collective-permute-start.3 = (bf16[4,128,256]{2,1,0:T(8,128)(2,1)S(1)}, bf16[4,128,256]{2,1,0:T(8,128)(2,1)S(1)}, u32[]{:S(2)}, u32[]{:S(2)}) collective-permute-start(bf16[4,128,256]{2,1,0:T(8,128)(2,1)S(1)} %pad_maximum_fusion.refs_10_), channel_id=1, source_target_pairs={{0,8},{4,36},{8,16},{12,44},{16,24},{20,52},{24,0},{28,60},{32,40}... | collective-permute-start | bytes 786440 | tf_op jit(solution)/shard_map/ppermute | solution.py:315
  16.6 9.0 %collective-permute-start.6 = (bf16[4,128,256]{2,1,0:T(8,128)(2,1)S(1)}, bf16[4,128,256]{2,1,0:T(8,128)(2,1)S(1)}, u32[]{:S(2)}, u32[]{:S(2)}) collective-permute-start(bf16[4,128,256]{2,1,0:T(8,128)(2,1)S(1)} %pad_maximum_fusion.refs_10_), channel_id=1, source_target_pairs={{0,4},{4,0},{8,12},{12,8},{16,20},{20,16},{24,28},{28,24},{32,36},... | collective-permute-start | bytes 786440 | tf_op jit(solution)/shard_map/ppermute | solution.py:318
  21.7 5.5 %copy-start.11 = (bf16[4,128,256]{2,1,0:T(8,128)(2,1)}, bf16[4,128,256]{2,1,0:T(8,128)(2,1)S(1)}, u32[]{:S(2)}) copy-start(bf16[4,128,256]{2,1,0:T(8,128)(2,1)S(1)} %collective-permute-done.5.refs_13_) | copy-start | bytes 786436
  21.7 4.0 %collective-permute-start.9 = (bf16[4,128,256]{2,1,0:T(8,128)(2,1)S(1)}, bf16[4,128,256]{2,1,0:T(8,128)(2,1)S(1)}, u32[]{:S(2)}, u32[]{:S(2)}) collective-permute-start(bf16[4,128,256]{2,1,0:T(8,128)(2,1)S(1)} %collective-permute-done.5.refs_13_), channel_id=1, source_target_pairs={{0,4},{4,0},{8,12},{12,8},{16,20},{20,16},{24,28},{28,24},{32,36},... | collective-permute-start | bytes 786440 | tf_op jit(solution)/shard_map/ppermute | solution.py:318
  22.9 4.3 %copy-start.12 = (bf16[4,128,256]{2,1,0:T(8,128)(2,1)}, bf16[4,128,256]{2,1,0:T(8,128)(2,1)S(1)}, u32[]{:S(2)}) copy-start(bf16[4,128,256]{2,1,0:T(8,128)(2,1)S(1)} %collective-permute-done.4.refs_12_) | copy-start | bytes 786436
  22.9 2.8 %collective-permute-start.8 = (bf16[4,128,256]{2,1,0:T(8,128)(2,1)S(1)}, bf16[4,128,256]{2,1,0:T(8,128)(2,1)S(1)}, u32[]{:S(2)}, u32[]{:S(2)}) collective-permute-start(bf16[4,128,256]{2,1,0:T(8,128)(2,1)S(1)} %collective-permute-done.4.refs_12_), channel_id=1, source_target_pairs={{0,4},{4,0},{8,12},{12,8},{16,20},{20,16},{24,28},{28,24},{32,36},... | collective-permute-start | bytes 786440 | tf_op jit(solution)/shard_map/ppermute | solution.py:318
  25.6 1.6 %copy-start.13 = (bf16[4,128,256]{2,1,0:T(8,128)(2,1)}, bf16[4,128,256]{2,1,0:T(8,128)(2,1)S(1)}, u32[]{:S(2)}) copy-start(bf16[4,128,256]{2,1,0:T(8,128)(2,1)S(1)} %collective-permute-done.3.refs_11_) | copy-start | bytes 786436
  25.6 1.5 %collective-permute-start.7 = (bf16[4,128,256]{2,1,0:T(8,128)(2,1)S(1)}, bf16[4,128,256]{2,1,0:T(8,128)(2,1)S(1)}, u32[]{:S(2)}, u32[]{:S(2)}) collective-permute-start(bf16[4,128,256]{2,1,0:T(8,128)(2,1)S(1)} %collective-permute-done.3.refs_11_), channel_id=1, source_target_pairs={{0,4},{4,0},{8,12},{12,8},{16,20},{20,16},{24,28},{28,24},{32,36},... | collective-permute-start | bytes 786440 | tf_op jit(solution)/shard_map/ppermute | solution.py:318
  25.7 1.6 %copy-start.14 = (bf16[4,128,256]{2,1,0:T(8,128)(2,1)}, bf16[4,128,256]{2,1,0:T(8,128)(2,1)S(1)}, u32[]{:S(2)}) copy-start(bf16[4,128,256]{2,1,0:T(8,128)(2,1)S(1)} %collective-permute-done.6.refs_14_) | copy-start | bytes 786436
  25.7 1.5 %copy-start.15 = (bf16[4,128,256]{2,1,0:T(8,128)(2,1)}, bf16[4,128,256]{2,1,0:T(8,128)(2,1)S(1)}, u32[]{:S(2)}) copy-start(bf16[4,128,256]{2,1,0:T(8,128)(2,1)S(1)} %collective-permute-done.9.refs_17_) | copy-start | bytes 786436
  25.7 1.5 %copy-start.16 = (bf16[4,128,256]{2,1,0:T(8,128)(2,1)}, bf16[4,128,256]{2,1,0:T(8,128)(2,1)S(1)}, u32[]{:S(2)}) copy-start(bf16[4,128,256]{2,1,0:T(8,128)(2,1)S(1)} %collective-permute-done.8.refs_16_) | copy-start | bytes 786436
  27.2 0.7 copy-start.17
  45.8 14.4 %collective-permute-start.16 = (s16[2112,256]{1,0:T(8,128)(2,1)}, s16[2112,256]{1,0:T(8,128)(2,1)S(1)}, u32[]{:S(2)}, u32[]{:S(2)}) collective-permute-start(s16[2112,256]{1,0:T(8,128)(2,1)} %get-tuple-element.57), channel_id=1, source_target_pairs={{0,4},{4,0},{8,12},{12,8},{16,20},{20,16},{24,28},{28,24},{32,36},... | collective-permute-start | bytes 3244040 | tf_op jit(solution)/shard_map/ppermute | solution.py:318
  52.5 17.6 %collective-permute-start.10 = (s16[528,256]{1,0:T(8,128)(2,1)}, s16[528,256]{1,0:T(8,128)(2,1)S(1)}, u32[]{:S(2)}, u32[]{:S(2)}) collective-permute-start(s16[528,256]{1,0:T(8,128)(2,1)} %get-tuple-element.53), channel_id=1, source_target_pairs={{0,3},{1,0},{2,1},{3,2},{4,7},{5,4},{6,5},{7,6},{8,11},{9,8},{10,9... | collective-permute-start | bytes 811016 | tf_op jit(solution)/shard_map/ppermute | solution.py:301
  57.7 12.5 %collective-permute-start.11 = (s16[528,256]{1,0:T(8,128)(2,1)}, s16[528,256]{1,0:T(8,128)(2,1)S(1)}, u32[]{:S(2)}, u32[]{:S(2)}) collective-permute-start(s16[528,256]{1,0:T(8,128)(2,1)} %get-tuple-element.54), channel_id=1, source_target_pairs={{0,2},{1,3},{2,0},{3,1},{4,6},{5,7},{6,4},{7,5},{8,10},{9,11},{10,... | collective-permute-start | bytes 811016 | tf_op jit(solution)/shard_map/ppermute | solution.py:301
  58.8 14.9 %collective-permute-start.12 = (s16[528,256]{1,0:T(8,128)(2,1)}, s16[528,256]{1,0:T(8,128)(2,1)S(1)}, u32[]{:S(2)}, u32[]{:S(2)}) collective-permute-start(s16[528,256]{1,0:T(8,128)(2,1)} %get-tuple-element.55), channel_id=1, source_target_pairs={{0,1},{1,2},{2,3},{3,0},{4,5},{5,6},{6,7},{7,4},{8,9},{9,10},{10,1... | collective-permute-start | bytes 811016 | tf_op jit(solution)/shard_map/ppermute | solution.py:301
  60.1 1.0 %copy-start = (s16[2112,256]{1,0:T(8,128)(2,1)}, s16[2112,256]{1,0:T(8,128)(2,1)S(1)}, u32[]{:S(2)}) copy-start(s16[2112,256]{1,0:T(8,128)(2,1)S(1)} %collective-permute-done.16.code_ref) | copy-start | bytes 3244036
  64.5 14.2 %collective-permute-start.17 = (s16[528,256]{1,0:T(8,128)(2,1)}, s16[528,256]{1,0:T(8,128)(2,1)S(1)}, u32[]{:S(2)}, u32[]{:S(2)}) collective-permute-start(s16[528,256]{1,0:T(8,128)(2,1)} %get-tuple-element.59), channel_id=1, source_target_pairs={{0,24},{4,100},{8,0},{12,108},{16,8},{20,116},{24,16},{28,124},{32... | collective-permute-start | bytes 811016 | tf_op jit(solution)/shard_map/ppermute | solution.py:315
  66.5 12.9 %collective-permute-start.18 = (s16[528,256]{1,0:T(8,128)(2,1)}, s16[528,256]{1,0:T(8,128)(2,1)S(1)}, u32[]{:S(2)}, u32[]{:S(2)}) collective-permute-start(s16[528,256]{1,0:T(8,128)(2,1)} %get-tuple-element.60), channel_id=1, source_target_pairs={{0,16},{4,68},{8,24},{12,76},{16,0},{20,84},{24,8},{28,92},{32,48}... | collective-permute-start | bytes 811016 | tf_op jit(solution)/shard_map/ppermute | solution.py:315
  70.1 3.6 %copy-start.2 = (s16[528,256]{1,0:T(8,128)(2,1)}, s16[528,256]{1,0:T(8,128)(2,1)S(1)}, u32[]{:S(2)}) copy-start(s16[528,256]{1,0:T(8,128)(2,1)S(1)} %collective-permute-done.10.p1) | copy-start | bytes 811012
  70.1 9.3 %collective-permute-start.19 = (s16[528,256]{1,0:T(8,128)(2,1)}, s16[528,256]{1,0:T(8,128)(2,1)S(1)}, u32[]{:S(2)}, u32[]{:S(2)}) collective-permute-start(s16[528,256]{1,0:T(8,128)(2,1)} %get-tuple-element.61), channel_id=1, source_target_pairs={{0,8},{4,36},{8,16},{12,44},{16,24},{20,52},{24,0},{28,60},{32,40}... | collective-permute-start | bytes 811016 | tf_op jit(solution)/shard_map/ppermute | solution.py:315
  70.1 3.6 %copy-start.3 = (s16[528,256]{1,0:T(8,128)(2,1)}, s16[528,256]{1,0:T(8,128)(2,1)S(1)}, u32[]{:S(2)}) copy-start(s16[528,256]{1,0:T(8,128)(2,1)S(1)} %collective-permute-done.11.p2) | copy-start | bytes 811012
  73.7 0.7 copy-start.4
  76.7 9.6 %collective-permute-start.15 = (s16[528,256]{1,0:T(8,128)(2,1)}, s16[528,256]{1,0:T(8,128)(2,1)S(1)}, u32[]{:S(2)}, u32[]{:S(2)}) collective-permute-start(s16[528,256]{1,0:T(8,128)(2,1)} %user_sum.1.p0), channel_id=1, source_target_pairs={{0,3},{1,0},{2,1},{3,2},{4,7},{5,4},{6,5},{7,6},{8,11},{9,8},{10,9... | collective-permute-start | bytes 811016 | tf_op jit(solution)/shard_map/ppermute | solution.py:301
  77.3 11.1 %collective-permute-start.14 = (s16[528,256]{1,0:T(8,128)(2,1)}, s16[528,256]{1,0:T(8,128)(2,1)S(1)}, u32[]{:S(2)}, u32[]{:S(2)}) collective-permute-start(s16[528,256]{1,0:T(8,128)(2,1)} %user_sum.1.p0), channel_id=1, source_target_pairs={{0,2},{1,3},{2,0},{3,1},{4,6},{5,7},{6,4},{7,5},{8,10},{9,11},{10,... | collective-permute-start | bytes 811016 | tf_op jit(solution)/shard_map/ppermute | solution.py:301
  78.7 0.8 copy-start.8
  78.7 14.0 %collective-permute-start.13 = (s16[528,256]{1,0:T(8,128)(2,1)}, s16[528,256]{1,0:T(8,128)(2,1)S(1)}, u32[]{:S(2)}, u32[]{:S(2)}) collective-permute-start(s16[528,256]{1,0:T(8,128)(2,1)} %user_sum.1.p0), channel_id=1, source_target_pairs={{0,1},{1,2},{2,3},{3,0},{4,5},{5,6},{6,7},{7,4},{8,9},{9,10},{10,1... | collective-permute-start | bytes 811016 | tf_op jit(solution)/shard_map/ppermute | solution.py:301
  79.5 0.7 copy-start.9
  79.5 0.8 copy-start.10
  82.5 10.1 %collective-permute-start.20 = (s16[144,256]{1,0:T(8,128)(2,1)}, s16[144,256]{1,0:T(8,128)(2,1)S(1)}, u32[]{:S(2)}, u32[]{:S(2)}) collective-permute-start(s16[144,256]{1,0:T(8,128)(2,1)} %get-tuple-element.63), channel_id=1, source_target_pairs={{0,96},{4,28},{8,104},{12,4},{16,112},{20,12},{24,120},{28,20},{32... | collective-permute-start | bytes 221192 | tf_op jit(solution)/shard_map/ppermute | solution.py:312
  82.6 10.1 %collective-permute-start.21 = (s16[144,256]{1,0:T(8,128)(2,1)}, s16[144,256]{1,0:T(8,128)(2,1)S(1)}, u32[]{:S(2)}, u32[]{:S(2)}) collective-permute-start(s16[144,256]{1,0:T(8,128)(2,1)} %get-tuple-element.64), channel_id=1, source_target_pairs={{0,64},{4,20},{8,72},{12,28},{16,80},{20,4},{24,88},{28,12},{32,96... | collective-permute-start | bytes 221192 | tf_op jit(solution)/shard_map/ppermute | solution.py:312
  86.3 7.3 %copy-start.5 = (s16[528,256]{1,0:T(8,128)(2,1)}, s16[528,256]{1,0:T(8,128)(2,1)S(1)}, u32[]{:S(2)}) copy-start(s16[528,256]{1,0:T(8,128)(2,1)S(1)} %collective-permute-done.15.p3) | copy-start | bytes 811012
  86.3 7.3 %collective-permute-start.22 = (s16[144,256]{1,0:T(8,128)(2,1)}, s16[144,256]{1,0:T(8,128)(2,1)S(1)}, u32[]{:S(2)}, u32[]{:S(2)}) collective-permute-start(s16[144,256]{1,0:T(8,128)(2,1)} %get-tuple-element.65), channel_id=1, source_target_pairs={{0,32},{4,12},{8,40},{12,20},{16,48},{20,28},{24,56},{28,4},{32,64... | collective-permute-start | bytes 221192 | tf_op jit(solution)/shard_map/ppermute | solution.py:312
  88.5 5.2 %copy-start.6 = (s16[528,256]{1,0:T(8,128)(2,1)}, s16[528,256]{1,0:T(8,128)(2,1)S(1)}, u32[]{:S(2)}) copy-start(s16[528,256]{1,0:T(8,128)(2,1)S(1)} %collective-permute-done.14.p2) | copy-start | bytes 811012
  92.7 1.0 %copy-start.7 = (s16[528,256]{1,0:T(8,128)(2,1)}, s16[528,256]{1,0:T(8,128)(2,1)S(1)}, u32[]{:S(2)}) copy-start(s16[528,256]{1,0:T(8,128)(2,1)S(1)} %collective-permute-done.13.p1) | copy-start | bytes 811012
  92.7 1.0 %copy-start.18 = (s16[144,256]{1,0:T(8,128)(2,1)}, s16[144,256]{1,0:T(8,128)(2,1)S(1)}, u32[]{:S(2)}) copy-start(s16[144,256]{1,0:T(8,128)(2,1)S(1)} %collective-permute-done.20.q1) | copy-start | bytes 221188
  92.7 1.0 %copy-start.19 = (s16[144,256]{1,0:T(8,128)(2,1)}, s16[144,256]{1,0:T(8,128)(2,1)S(1)}, u32[]{:S(2)}) copy-start(s16[144,256]{1,0:T(8,128)(2,1)S(1)} %collective-permute-done.21.q2) | copy-start | bytes 221188
  93.6 0.6 copy-start.20
